TPU v7x, 256 devices: a whole 4x4x8 slice. The times are simulated.
256 devices in a mesh: ctx: 64 (over z, x, y_lo), head: 4 (over y_hi, core).
Axes of the slice: x: 4, y: 4 (y_hi: 2, y_lo: 2; y = y_hi * 2 + y_lo), z: 8, core: 2. Of those that a mesh axis runs over, the one named last changes fastest.
Arguments:
- queries: bfloat16 [8192, 2048], P(('ctx', 'head')), as said below
- key_rows: bfloat16 [8192, 512], P(('ctx', 'head')), as said below
- value_rows: bfloat16 [8192, 512], P(('ctx', 'head')), may hold values from -6 to 6
- query_tangent: bfloat16 [8192, 2048], P(('ctx', 'head')), may hold values from -6 to 6
- key_tangent: bfloat16 [8192, 512], P(('ctx', 'head')), may hold values from -6 to 6
- value_tangent: bfloat16 [8192, 512], P(('ctx', 'head')), may hold values from -6 to 6
- block_plan: int32 [64], replicated, may hold values from 0 to 63, each once
- block_docs: int32 [64], replicated, may hold values from 0 to 15, never falling along the last dimension, each value on 1 to 8 neighbouring positions
Outputs:
- attended: bfloat16 [8192, 2048], P(('ctx', 'head'))
- attended_tangent: bfloat16 [8192, 2048], P(('ctx', 'head'))
Inputs may be any that keep to these rules, and one draw needn't show every extreme that they name: `block_plan`: each packed block holds a different context block. `block_docs`: ids never fall along the context; each document covers 1 to 8 blocks, one exactly 8. `queries`: entries lie within -6 and 6. `key_rows`: entries lie within -6 and 6.
All inputs are finite; a program needn't handle non-finite values.
Results may differ from a plain program's by a relative error of at most 0.0083.
Values may be sent and summed in bfloat16 or wider, within the bound.
No kernel may reach another device: no remote copies, remote signals or barrier semaphores. Data moves between devices by JAX's collectives and lax.ppermute only.
A program may use at most 128 MiB of HBM per device.

v0:
```python
import math

import jax
import jax.numpy as jnp
from jax import lax
from jax.sharding import PartitionSpec as P

HD = 128
BLK = 128


def passed_along(value, axis, steps):
    count = lax.axis_size(axis)
    pairs = [(source, (source + steps) % count) for source in range(count)]
    return lax.ppermute(value, axis, pairs)


def on_device(
    queries, key_rows, value_rows, query_tangent, key_tangent, value_tangent, block_plan, block_docs
):
    query, keys, values, qtan, ktan, vtan = (
        lax.all_to_all(queries, "head", split_axis=1, concat_axis=0, tiled=True),
        lax.all_to_all(key_rows, "head", split_axis=1, concat_axis=0, tiled=True),
        lax.all_to_all(value_rows, "head", split_axis=1, concat_axis=0, tiled=True),
        lax.all_to_all(query_tangent, "head", split_axis=1, concat_axis=0, tiled=True),
        lax.all_to_all(key_tangent, "head", split_axis=1, concat_axis=0, tiled=True),
        lax.all_to_all(value_tangent, "head", split_axis=1, concat_axis=0, tiled=True),
    )
    scale = 1.0 / math.sqrt(HD)
    rows = query.shape[0]
    heads = query.shape[1] // HD
    kv_local = keys.shape[1] // HD
    group = heads // kv_local
    blocks_per = rows // BLK
    shards = lax.axis_size("ctx")
    myself = lax.axis_index("ctx")
    query4 = query.reshape(rows, kv_local, group, HD)
    qtan4 = qtan.reshape(rows, kv_local, group, HD)

    def positions(shard, start, count):
        local = start + jnp.arange(count, dtype=jnp.int32)
        placed = jnp.take(block_plan, shard * blocks_per + local // BLK)
        return (placed * BLK + local % BLK, jnp.take(block_docs, placed))

    qpos, qdoc = positions(myself, 0, rows)

    def visible(shard, start, count):
        kpos, kdoc = positions(shard, start, count)
        return (qdoc[:, None] == kdoc[None, :]) & (kpos[None, :] <= qpos[:, None])

    def absorb_masked(state, stacked, mask):
        top, total, curve, acc_a, acc_b = state
        count = stacked.shape[1]
        keyb = stacked[0].reshape(count, kv_local, HD)
        valb = stacked[1].reshape(count, kv_local, HD)
        ktanb = stacked[2].reshape(count, kv_local, HD)
        vtanb = stacked[3].reshape(count, kv_local, HD)
        score = (
            jnp.einsum("qhgd,khd->hgqk", query4, keyb, preferred_element_type=jnp.float32) * scale
        )
        dscore = (
            jnp.einsum("qhgd,khd->hgqk", qtan4, keyb, preferred_element_type=jnp.float32)
            + jnp.einsum("qhgd,khd->hgqk", query4, ktanb, preferred_element_type=jnp.float32)
        ) * scale
        wide_mask = mask[None, None]
        masked = jnp.where(wide_mask, score, -1e30)
        top_new = jnp.maximum(top, jnp.max(masked, axis=-1))
        factor = jnp.exp(top - top_new)
        weight = jnp.where(wide_mask, jnp.exp(masked - top_new[..., None]), 0.0)
        total = factor * total + jnp.sum(weight, axis=-1)
        curve = factor * curve + jnp.sum(weight * dscore, axis=-1)
        weight_b = weight.astype(jnp.bfloat16)
        wds_b = (weight * dscore).astype(jnp.bfloat16)
        factor_q = jnp.transpose(factor, (2, 0, 1))[..., None]
        acc_a = factor_q * acc_a + jnp.einsum(
            "hgqk,khd->qhgd", weight_b, valb, preferred_element_type=jnp.float32
        )
        acc_b = (
            factor_q * acc_b
            + jnp.einsum("hgqk,khd->qhgd", wds_b, valb, preferred_element_type=jnp.float32)
            + jnp.einsum("hgqk,khd->qhgd", weight_b, vtanb, preferred_element_type=jnp.float32)
        )
        return (top_new, total, curve, acc_a, acc_b)

    def absorb(state, stacked, shard, start):
        return absorb_masked(state, stacked, visible(shard, start, stacked.shape[1]))

    state = (
        jnp.full((kv_local, group, rows), -1e30, jnp.float32),
        jnp.zeros((kv_local, group, rows), jnp.float32),
        jnp.zeros((kv_local, group, rows), jnp.float32),
        jnp.zeros((rows, kv_local, group, HD), jnp.float32),
        jnp.zeros((rows, kv_local, group, HD), jnp.float32),
    )
    stacked = jnp.stack([keys, values, ktan, vtan])

    def one_turn(turn, carry):
        current, moving = carry
        current = absorb(current, moving, (myself - turn) % shards, 0)
        moving = passed_along(moving, "ctx", 1)
        return (current, moving)

    state, stacked = lax.fori_loop(0, shards - 1, one_turn, (state, stacked))
    state = absorb(state, stacked, (myself - (shards - 1)) % shards, 0)
    top, total, curve, acc_a, acc_b = state
    total_q = jnp.transpose(total, (2, 0, 1))[..., None]
    curve_q = jnp.transpose(curve, (2, 0, 1))[..., None]
    output = acc_a / total_q
    tangent = acc_b / total_q - curve_q / total_q * output
    output_b = output.astype(jnp.bfloat16).reshape(rows, heads * HD)
    tangent_b = tangent.astype(jnp.bfloat16).reshape(rows, heads * HD)
    attended, attended_tangent = (
        lax.all_to_all(output_b, "head", split_axis=0, concat_axis=1, tiled=True),
        lax.all_to_all(tangent_b, "head", split_axis=0, concat_axis=1, tiled=True),
    )
    return (attended, attended_tangent)


def solution(mesh):
    placed = (
        P(("ctx", "head"), None),
        P(("ctx", "head"), None),
        P(("ctx", "head"), None),
        P(("ctx", "head"), None),
        P(("ctx", "head"), None),
        P(("ctx", "head"), None),
        P(),
        P(),
    )
    return jax.shard_map(
        on_device,
        mesh=mesh,
        in_specs=placed,
        out_specs=(P(("ctx", "head"), None), P(("ctx", "head"), None)),
        check_vma=False,
    )
```

profile of v0, /device:TPU:1, one launch (start us, length us, event | category | flops | bytes accessed | tf_op | source)
XLA Modules:
  0.0 681.0 jit_solution(16811387818887698039)
XLA Ops:
  2.0 6.6 all-to-all-start.3
  15.2 4.8 all-to-all-start.2
  20.1 4.7 all-to-all-done.2
  24.7 4.0 all-to-all-start.1
  33.4 4.0 all-to-all-start
  38.1 4.0 all-to-all-done
  42.1 4.2 all-to-all-start.5
  47.1 4.3 all-to-all-done.5
  51.4 4.3 all-to-all-start.4
  55.8 5.0 all-to-all-done.4
  61.0 529.6 %while.27 = (s32[]{:T(128)}, f32[1,4,128]{2,1,0:T(4,128)S(1)}, f32[1,4,128]{2,1,0:T(4,128)S(1)}, f32[1,4,128]{2,1,0:T(4,128)S(1)}, f32[128,1,4,128]{3,0,2,1:T(8,...) while((s32[]{:T(128)}, f32[1,4,128]{2,1,0:T(4,128)S(1)}, ...), condition=%wide.region_4.6_spmd.clone, body=%wide.region_0.5_spmd.clone.sunk | while | flops 102428432 | bytes 5210459 | solution.py:103
  65.3 6.0 collective-permute-done
  83.7 3.8 collective-permute-done
  116.2 3.8 collective-permute-done
  124.3 5.0 collective-permute-done
  133.6 4.7 collective-permute-done
  167.0 3.8 collective-permute-done
  191.4 4.5 collective-permute-done
  200.2 5.1 collective-permute-done
  209.6 4.2 collective-permute-done
  226.2 3.8 collective-permute-done
  258.8 3.9 collective-permute-done
  266.9 5.0 collective-permute-done
  276.3 4.7 collective-permute-done
  301.5 3.8 collective-permute-done
  309.6 3.8 collective-permute-done
  334.0 4.5 collective-permute-done
  342.9 5.1 collective-permute-done
  352.3 4.2 collective-permute-done
  368.9 3.8 collective-permute-done
  401.4 3.9 collective-permute-done
  409.6 5.0 collective-permute-done
  418.9 4.7 collective-permute-done
  444.1 3.8 collective-permute-done
  476.7 4.5 collective-permute-done
  485.5 5.1 collective-permute-done
  494.9 4.2 collective-permute-done
  503.4 3.8 collective-permute-done
  511.5 3.8 collective-permute-done
  535.9 3.8 collective-permute-done
  544.0 3.9 collective-permute-done
  552.2 5.0 collective-permute-done
  561.5 4.7 collective-permute-done
  586.8 3.8 collective-permute-done
  592.9 72.9 %all-to-all-start.6 = ((bf16[4,32,512]{2,1,0:T(8,128)(2,1)}), bf16[4,32,512]{2,1,0:T(8,128)(2,1)S(1)}, u32[]{:S(2)}, u32[]{:S(2)}) async-start(bf16[4,32,512]{2,1,0:T(8,128)(2,1)} %all_to_all.118), calls=%async_computation.6 | async-start | bytes 262144 | tf_op jit(solution)/shard_map/all_to_all | solution.py:113
  667.0 3.9 all-to-all-done.6
  670.9 4.3 all-to-all-start.7
  675.9 4.4 all-to-all-done.7
  (1360 shorter events, 395.3 us)
Async XLA Ops:
  2.0 13.2 %all-to-all-start.3 = ((bf16[32,4,128]{2,0,1:T(8,128)(2,1)}), bf16[32,4,128]{2,0,1:T(8,128)(2,1)S(1)}, u32[]{:S(2)}, u32[]{:S(2)}) async-start(bf16[32,4,128]{2,0,1:T(8,128)(2,1)} %copy_bitcast_fusion.2), calls=%async_computation.3 | async-start | bytes 65536 | tf_op jit(solution)/shard_map/all_to_all | solution.py:27
  15.2 9.5 %all-to-all-start.2 = ((bf16[32,4,128]{2,0,1:T(8,128)(2,1)}), bf16[32,4,128]{2,0,1:T(8,128)(2,1)S(1)}, u32[]{:S(2)}, u32[]{:S(2)}) async-start(bf16[32,4,128]{2,0,1:T(8,128)(2,1)} %copy_bitcast_fusion.3), calls=%async_computation.2 | async-start | bytes 65536 | tf_op jit(solution)/shard_map/all_to_all | solution.py:26
  24.7 8.7 %all-to-all-start.1 = ((bf16[32,4,128]{2,0,1:T(8,128)(2,1)}), bf16[32,4,128]{2,0,1:T(8,128)(2,1)S(1)}, u32[]{:S(2)}, u32[]{:S(2)}) async-start(bf16[32,4,128]{2,0,1:T(8,128)(2,1)} %copy_bitcast_fusion.4), calls=%async_computation.1 | async-start | bytes 65536 | tf_op jit(solution)/shard_map/all_to_all | solution.py:24
  33.4 8.7 %all-to-all-start = ((bf16[32,4,128]{2,0,1:T(8,128)(2,1)}), bf16[32,4,128]{2,0,1:T(8,128)(2,1)S(1)}, u32[]{:S(2)}, u32[]{:S(2)}) async-start(bf16[32,4,128]{2,0,1:T(8,128)(2,1)} %copy_bitcast_fusion.5), calls=%async_computation | async-start | bytes 65536 | tf_op jit(solution)/shard_map/all_to_all | solution.py:23
  42.1 9.3 %all-to-all-start.5 = ((bf16[32,4,512]{2,0,1:T(8,128)(2,1)}), bf16[32,4,512]{2,0,1:T(8,128)(2,1)S(1)}, u32[]{:S(2)}, u32[]{:S(2)}) async-start(bf16[32,4,512]{2,0,1:T(8,128)(2,1)} %bitcast.250), calls=%async_computation.5 | async-start | bytes 262144 | tf_op jit(solution)/shard_map/all_to_all | solution.py:25
  51.4 9.4 %all-to-all-start.4 = ((bf16[32,4,512]{2,0,1:T(8,128)(2,1)}), bf16[32,4,512]{2,0,1:T(8,128)(2,1)S(1)}, u32[]{:S(2)}, u32[]{:S(2)}) async-start(bf16[32,4,512]{2,0,1:T(8,128)(2,1)} %bitcast.251), calls=%async_computation.4 | async-start | bytes 262144 | tf_op jit(solution)/shard_map/all_to_all | solution.py:22
  61.0 10.3 %collective-permute-start = (bf16[4,128,128]{2,1,0:T(8,128)(2,1)S(1)}, bf16[4,128,128]{2,1,0:T(8,128)(2,1)S(1)}, u32[]{:S(2)}, u32[]{:S(2)}) collective-permute-start(bf16[4,128,128]{2,1,0:T(8,128)(2,1)S(1)} %copy.119), channel_id=1, source_target_pairs={{0,4},{4,8},{8,12},{12,16},{16,20},{20,24},{24,28},{28,32},{32,36}... | collective-permute-start | bytes 393224 | tf_op jit(solution)/shard_map/while/body/eval_jaxpr/ppermute | solution.py:15
  71.3 8.1 %collective-permute-start = (bf16[4,128,128]{2,1,0:T(8,128)(2,1)S(1)}, bf16[4,128,128]{2,1,0:T(8,128)(2,1)S(1)}, u32[]{:S(2)}, u32[]{:S(2)}) collective-permute-start(bf16[4,128,128]{2,1,0:T(8,128)(2,1)S(1)} %copy.119), channel_id=1, source_target_pairs={{0,4},{4,8},{8,12},{12,16},{16,20},{20,24},{24,28},{28,32},{32,36}... | collective-permute-start | bytes 393224 | tf_op jit(solution)/shard_map/while/body/eval_jaxpr/ppermute | solution.py:15
  79.4 8.1 %collective-permute-start = (bf16[4,128,128]{2,1,0:T(8,128)(2,1)S(1)}, bf16[4,128,128]{2,1,0:T(8,128)(2,1)S(1)}, u32[]{:S(2)}, u32[]{:S(2)}) collective-permute-start(bf16[4,128,128]{2,1,0:T(8,128)(2,1)S(1)} %copy.119), channel_id=1, source_target_pairs={{0,4},{4,8},{8,12},{12,16},{16,20},{20,24},{24,28},{28,32},{32,36}... | collective-permute-start | bytes 393224 | tf_op jit(solution)/shard_map/while/body/eval_jaxpr/ppermute | solution.py:15
  87.5 8.1 %collective-permute-start = (bf16[4,128,128]{2,1,0:T(8,128)(2,1)S(1)}, bf16[4,128,128]{2,1,0:T(8,128)(2,1)S(1)}, u32[]{:S(2)}, u32[]{:S(2)}) collective-permute-start(bf16[4,128,128]{2,1,0:T(8,128)(2,1)S(1)} %copy.119), channel_id=1, source_target_pairs={{0,4},{4,8},{8,12},{12,16},{16,20},{20,24},{24,28},{28,32},{32,36}... | collective-permute-start | bytes 393224 | tf_op jit(solution)/shard_map/while/body/eval_jaxpr/ppermute | solution.py:15
  95.7 8.1 %collective-permute-start = (bf16[4,128,128]{2,1,0:T(8,128)(2,1)S(1)}, bf16[4,128,128]{2,1,0:T(8,128)(2,1)S(1)}, u32[]{:S(2)}, u32[]{:S(2)}) collective-permute-start(bf16[4,128,128]{2,1,0:T(8,128)(2,1)S(1)} %copy.119), channel_id=1, source_target_pairs={{0,4},{4,8},{8,12},{12,16},{16,20},{20,24},{24,28},{28,32},{32,36}... | collective-permute-start | bytes 393224 | tf_op jit(solution)/shard_map/while/body/eval_jaxpr/ppermute | solution.py:15
  103.8 8.1 %collective-permute-start = (bf16[4,128,128]{2,1,0:T(8,128)(2,1)S(1)}, bf16[4,128,128]{2,1,0:T(8,128)(2,1)S(1)}, u32[]{:S(2)}, u32[]{:S(2)}) collective-permute-start(bf16[4,128,128]{2,1,0:T(8,128)(2,1)S(1)} %copy.119), channel_id=1, source_target_pairs={{0,4},{4,8},{8,12},{12,16},{16,20},{20,24},{24,28},{28,32},{32,36}... | collective-permute-start | bytes 393224 | tf_op jit(solution)/shard_map/while/body/eval_jaxpr/ppermute | solution.py:15
  111.9 8.1 %collective-permute-start = (bf16[4,128,128]{2,1,0:T(8,128)(2,1)S(1)}, bf16[4,128,128]{2,1,0:T(8,128)(2,1)S(1)}, u32[]{:S(2)}, u32[]{:S(2)}) collective-permute-start(bf16[4,128,128]{2,1,0:T(8,128)(2,1)S(1)} %copy.119), channel_id=1, source_target_pairs={{0,4},{4,8},{8,12},{12,16},{16,20},{20,24},{24,28},{28,32},{32,36}... | collective-permute-start | bytes 393224 | tf_op jit(solution)/shard_map/while/body/eval_jaxpr/ppermute | solution.py:15
  120.1 9.3 %collective-permute-start = (bf16[4,128,128]{2,1,0:T(8,128)(2,1)S(1)}, bf16[4,128,128]{2,1,0:T(8,128)(2,1)S(1)}, u32[]{:S(2)}, u32[]{:S(2)}) collective-permute-start(bf16[4,128,128]{2,1,0:T(8,128)(2,1)S(1)} %copy.119), channel_id=1, source_target_pairs={{0,4},{4,8},{8,12},{12,16},{16,20},{20,24},{24,28},{28,32},{32,36}... | collective-permute-start | bytes 393224 | tf_op jit(solution)/shard_map/while/body/eval_jaxpr/ppermute | solution.py:15
  129.3 9.0 %collective-permute-start = (bf16[4,128,128]{2,1,0:T(8,128)(2,1)S(1)}, bf16[4,128,128]{2,1,0:T(8,128)(2,1)S(1)}, u32[]{:S(2)}, u32[]{:S(2)}) collective-permute-start(bf16[4,128,128]{2,1,0:T(8,128)(2,1)S(1)} %copy.119), channel_id=1, source_target_pairs={{0,4},{4,8},{8,12},{12,16},{16,20},{20,24},{24,28},{28,32},{32,36}... | collective-permute-start | bytes 393224 | tf_op jit(solution)/shard_map/while/body/eval_jaxpr/ppermute | solution.py:15
  138.3 8.1 %collective-permute-start = (bf16[4,128,128]{2,1,0:T(8,128)(2,1)S(1)}, bf16[4,128,128]{2,1,0:T(8,128)(2,1)S(1)}, u32[]{:S(2)}, u32[]{:S(2)}) collective-permute-start(bf16[4,128,128]{2,1,0:T(8,128)(2,1)S(1)} %copy.119), channel_id=1, source_target_pairs={{0,4},{4,8},{8,12},{12,16},{16,20},{20,24},{24,28},{28,32},{32,36}... | collective-permute-start | bytes 393224 | tf_op jit(solution)/shard_map/while/body/eval_jaxpr/ppermute | solution.py:15
  146.4 8.1 %collective-permute-start = (bf16[4,128,128]{2,1,0:T(8,128)(2,1)S(1)}, bf16[4,128,128]{2,1,0:T(8,128)(2,1)S(1)}, u32[]{:S(2)}, u32[]{:S(2)}) collective-permute-start(bf16[4,128,128]{2,1,0:T(8,128)(2,1)S(1)} %copy.119), channel_id=1, source_target_pairs={{0,4},{4,8},{8,12},{12,16},{16,20},{20,24},{24,28},{28,32},{32,36}... | collective-permute-start | bytes 393224 | tf_op jit(solution)/shard_map/while/body/eval_jaxpr/ppermute | solution.py:15
  154.6 8.1 %collective-permute-start = (bf16[4,128,128]{2,1,0:T(8,128)(2,1)S(1)}, bf16[4,128,128]{2,1,0:T(8,128)(2,1)S(1)}, u32[]{:S(2)}, u32[]{:S(2)}) collective-permute-start(bf16[4,128,128]{2,1,0:T(8,128)(2,1)S(1)} %copy.119), channel_id=1, source_target_pairs={{0,4},{4,8},{8,12},{12,16},{16,20},{20,24},{24,28},{28,32},{32,36}... | collective-permute-start | bytes 393224 | tf_op jit(solution)/shard_map/while/body/eval_jaxpr/ppermute | solution.py:15
  162.7 8.1 %collective-permute-start = (bf16[4,128,128]{2,1,0:T(8,128)(2,1)S(1)}, bf16[4,128,128]{2,1,0:T(8,128)(2,1)S(1)}, u32[]{:S(2)}, u32[]{:S(2)}) collective-permute-start(bf16[4,128,128]{2,1,0:T(8,128)(2,1)S(1)} %copy.119), channel_id=1, source_target_pairs={{0,4},{4,8},{8,12},{12,16},{16,20},{20,24},{24,28},{28,32},{32,36}... | collective-permute-start | bytes 393224 | tf_op jit(solution)/shard_map/while/body/eval_jaxpr/ppermute | solution.py:15
  170.8 8.1 %collective-permute-start = (bf16[4,128,128]{2,1,0:T(8,128)(2,1)S(1)}, bf16[4,128,128]{2,1,0:T(8,128)(2,1)S(1)}, u32[]{:S(2)}, u32[]{:S(2)}) collective-permute-start(bf16[4,128,128]{2,1,0:T(8,128)(2,1)S(1)} %copy.119), channel_id=1, source_target_pairs={{0,4},{4,8},{8,12},{12,16},{16,20},{20,24},{24,28},{28,32},{32,36}... | collective-permute-start | bytes 393224 | tf_op jit(solution)/shard_map/while/body/eval_jaxpr/ppermute | solution.py:15
  179.0 8.1 %collective-permute-start = (bf16[4,128,128]{2,1,0:T(8,128)(2,1)S(1)}, bf16[4,128,128]{2,1,0:T(8,128)(2,1)S(1)}, u32[]{:S(2)}, u32[]{:S(2)}) collective-permute-start(bf16[4,128,128]{2,1,0:T(8,128)(2,1)S(1)} %copy.119), channel_id=1, source_target_pairs={{0,4},{4,8},{8,12},{12,16},{16,20},{20,24},{24,28},{28,32},{32,36}... | collective-permute-start | bytes 393224 | tf_op jit(solution)/shard_map/while/body/eval_jaxpr/ppermute | solution.py:15
  187.1 8.8 %collective-permute-start = (bf16[4,128,128]{2,1,0:T(8,128)(2,1)S(1)}, bf16[4,128,128]{2,1,0:T(8,128)(2,1)S(1)}, u32[]{:S(2)}, u32[]{:S(2)}) collective-permute-start(bf16[4,128,128]{2,1,0:T(8,128)(2,1)S(1)} %copy.119), channel_id=1, source_target_pairs={{0,4},{4,8},{8,12},{12,16},{16,20},{20,24},{24,28},{28,32},{32,36}... | collective-permute-start | bytes 393224 | tf_op jit(solution)/shard_map/while/body/eval_jaxpr/ppermute | solution.py:15
  195.9 9.4 %collective-permute-start = (bf16[4,128,128]{2,1,0:T(8,128)(2,1)S(1)}, bf16[4,128,128]{2,1,0:T(8,128)(2,1)S(1)}, u32[]{:S(2)}, u32[]{:S(2)}) collective-permute-start(bf16[4,128,128]{2,1,0:T(8,128)(2,1)S(1)} %copy.119), channel_id=1, source_target_pairs={{0,4},{4,8},{8,12},{12,16},{16,20},{20,24},{24,28},{28,32},{32,36}... | collective-permute-start | bytes 393224 | tf_op jit(solution)/shard_map/while/body/eval_jaxpr/ppermute | solution.py:15
  205.3 8.5 %collective-permute-start = (bf16[4,128,128]{2,1,0:T(8,128)(2,1)S(1)}, bf16[4,128,128]{2,1,0:T(8,128)(2,1)S(1)}, u32[]{:S(2)}, u32[]{:S(2)}) collective-permute-start(bf16[4,128,128]{2,1,0:T(8,128)(2,1)S(1)} %copy.119), channel_id=1, source_target_pairs={{0,4},{4,8},{8,12},{12,16},{16,20},{20,24},{24,28},{28,32},{32,36}... | collective-permute-start | bytes 393224 | tf_op jit(solution)/shard_map/while/body/eval_jaxpr/ppermute | solution.py:15
  213.8 8.1 %collective-permute-start = (bf16[4,128,128]{2,1,0:T(8,128)(2,1)S(1)}, bf16[4,128,128]{2,1,0:T(8,128)(2,1)S(1)}, u32[]{:S(2)}, u32[]{:S(2)}) collective-permute-start(bf16[4,128,128]{2,1,0:T(8,128)(2,1)S(1)} %copy.119), channel_id=1, source_target_pairs={{0,4},{4,8},{8,12},{12,16},{16,20},{20,24},{24,28},{28,32},{32,36}... | collective-permute-start | bytes 393224 | tf_op jit(solution)/shard_map/while/body/eval_jaxpr/ppermute | solution.py:15
  222.0 8.1 %collective-permute-start = (bf16[4,128,128]{2,1,0:T(8,128)(2,1)S(1)}, bf16[4,128,128]{2,1,0:T(8,128)(2,1)S(1)}, u32[]{:S(2)}, u32[]{:S(2)}) collective-permute-start(bf16[4,128,128]{2,1,0:T(8,128)(2,1)S(1)} %copy.119), channel_id=1, source_target_pairs={{0,4},{4,8},{8,12},{12,16},{16,20},{20,24},{24,28},{28,32},{32,36}... | collective-permute-start | bytes 393224 | tf_op jit(solution)/shard_map/while/body/eval_jaxpr/ppermute | solution.py:15
  230.1 8.1 %collective-permute-start = (bf16[4,128,128]{2,1,0:T(8,128)(2,1)S(1)}, bf16[4,128,128]{2,1,0:T(8,128)(2,1)S(1)}, u32[]{:S(2)}, u32[]{:S(2)}) collective-permute-start(bf16[4,128,128]{2,1,0:T(8,128)(2,1)S(1)} %copy.119), channel_id=1, source_target_pairs={{0,4},{4,8},{8,12},{12,16},{16,20},{20,24},{24,28},{28,32},{32,36}... | collective-permute-start | bytes 393224 | tf_op jit(solution)/shard_map/while/body/eval_jaxpr/ppermute | solution.py:15
  238.2 8.1 %collective-permute-start = (bf16[4,128,128]{2,1,0:T(8,128)(2,1)S(1)}, bf16[4,128,128]{2,1,0:T(8,128)(2,1)S(1)}, u32[]{:S(2)}, u32[]{:S(2)}) collective-permute-start(bf16[4,128,128]{2,1,0:T(8,128)(2,1)S(1)} %copy.119), channel_id=1, source_target_pairs={{0,4},{4,8},{8,12},{12,16},{16,20},{20,24},{24,28},{28,32},{32,36}... | collective-permute-start | bytes 393224 | tf_op jit(solution)/shard_map/while/body/eval_jaxpr/ppermute | solution.py:15
  246.3 8.1 %collective-permute-start = (bf16[4,128,128]{2,1,0:T(8,128)(2,1)S(1)}, bf16[4,128,128]{2,1,0:T(8,128)(2,1)S(1)}, u32[]{:S(2)}, u32[]{:S(2)}) collective-permute-start(bf16[4,128,128]{2,1,0:T(8,128)(2,1)S(1)} %copy.119), channel_id=1, source_target_pairs={{0,4},{4,8},{8,12},{12,16},{16,20},{20,24},{24,28},{28,32},{32,36}... | collective-permute-start | bytes 393224 | tf_op jit(solution)/shard_map/while/body/eval_jaxpr/ppermute | solution.py:15
  254.5 8.2 %collective-permute-start = (bf16[4,128,128]{2,1,0:T(8,128)(2,1)S(1)}, bf16[4,128,128]{2,1,0:T(8,128)(2,1)S(1)}, u32[]{:S(2)}, u32[]{:S(2)}) collective-permute-start(bf16[4,128,128]{2,1,0:T(8,128)(2,1)S(1)} %copy.119), channel_id=1, source_target_pairs={{0,4},{4,8},{8,12},{12,16},{16,20},{20,24},{24,28},{28,32},{32,36}... | collective-permute-start | bytes 393224 | tf_op jit(solution)/shard_map/while/body/eval_jaxpr/ppermute | solution.py:15
  262.7 9.3 %collective-permute-start = (bf16[4,128,128]{2,1,0:T(8,128)(2,1)S(1)}, bf16[4,128,128]{2,1,0:T(8,128)(2,1)S(1)}, u32[]{:S(2)}, u32[]{:S(2)}) collective-permute-start(bf16[4,128,128]{2,1,0:T(8,128)(2,1)S(1)} %copy.119), channel_id=1, source_target_pairs={{0,4},{4,8},{8,12},{12,16},{16,20},{20,24},{24,28},{28,32},{32,36}... | collective-permute-start | bytes 393224 | tf_op jit(solution)/shard_map/while/body/eval_jaxpr/ppermute | solution.py:15
  272.0 9.0 %collective-permute-start = (bf16[4,128,128]{2,1,0:T(8,128)(2,1)S(1)}, bf16[4,128,128]{2,1,0:T(8,128)(2,1)S(1)}, u32[]{:S(2)}, u32[]{:S(2)}) collective-permute-start(bf16[4,128,128]{2,1,0:T(8,128)(2,1)S(1)} %copy.119), channel_id=1, source_target_pairs={{0,4},{4,8},{8,12},{12,16},{16,20},{20,24},{24,28},{28,32},{32,36}... | collective-permute-start | bytes 393224 | tf_op jit(solution)/shard_map/while/body/eval_jaxpr/ppermute | solution.py:15
  289.1 8.1 %collective-permute-start = (bf16[4,128,128]{2,1,0:T(8,128)(2,1)S(1)}, bf16[4,128,128]{2,1,0:T(8,128)(2,1)S(1)}, u32[]{:S(2)}, u32[]{:S(2)}) collective-permute-start(bf16[4,128,128]{2,1,0:T(8,128)(2,1)S(1)} %copy.119), channel_id=1, source_target_pairs={{0,4},{4,8},{8,12},{12,16},{16,20},{20,24},{24,28},{28,32},{32,36}... | collective-permute-start | bytes 393224 | tf_op jit(solution)/shard_map/while/body/eval_jaxpr/ppermute | solution.py:15
  297.2 8.1 %collective-permute-start = (bf16[4,128,128]{2,1,0:T(8,128)(2,1)S(1)}, bf16[4,128,128]{2,1,0:T(8,128)(2,1)S(1)}, u32[]{:S(2)}, u32[]{:S(2)}) collective-permute-start(bf16[4,128,128]{2,1,0:T(8,128)(2,1)S(1)} %copy.119), channel_id=1, source_target_pairs={{0,4},{4,8},{8,12},{12,16},{16,20},{20,24},{24,28},{28,32},{32,36}... | collective-permute-start | bytes 393224 | tf_op jit(solution)/shard_map/while/body/eval_jaxpr/ppermute | solution.py:15
  329.7 8.8 %collective-permute-start = (bf16[4,128,128]{2,1,0:T(8,128)(2,1)S(1)}, bf16[4,128,128]{2,1,0:T(8,128)(2,1)S(1)}, u32[]{:S(2)}, u32[]{:S(2)}) collective-permute-start(bf16[4,128,128]{2,1,0:T(8,128)(2,1)S(1)} %copy.119), channel_id=1, source_target_pairs={{0,4},{4,8},{8,12},{12,16},{16,20},{20,24},{24,28},{28,32},{32,36}... | collective-permute-start | bytes 393224 | tf_op jit(solution)/shard_map/while/body/eval_jaxpr/ppermute | solution.py:15
  338.6 9.4 %collective-permute-start = (bf16[4,128,128]{2,1,0:T(8,128)(2,1)S(1)}, bf16[4,128,128]{2,1,0:T(8,128)(2,1)S(1)}, u32[]{:S(2)}, u32[]{:S(2)}) collective-permute-start(bf16[4,128,128]{2,1,0:T(8,128)(2,1)S(1)} %copy.119), channel_id=1, source_target_pairs={{0,4},{4,8},{8,12},{12,16},{16,20},{20,24},{24,28},{28,32},{32,36}... | collective-permute-start | bytes 393224 | tf_op jit(solution)/shard_map/while/body/eval_jaxpr/ppermute | solution.py:15
  348.0 8.5 %collective-permute-start = (bf16[4,128,128]{2,1,0:T(8,128)(2,1)S(1)}, bf16[4,128,128]{2,1,0:T(8,128)(2,1)S(1)}, u32[]{:S(2)}, u32[]{:S(2)}) collective-permute-start(bf16[4,128,128]{2,1,0:T(8,128)(2,1)S(1)} %copy.119), channel_id=1, source_target_pairs={{0,4},{4,8},{8,12},{12,16},{16,20},{20,24},{24,28},{28,32},{32,36}... | collective-permute-start | bytes 393224 | tf_op jit(solution)/shard_map/while/body/eval_jaxpr/ppermute | solution.py:15
  397.1 8.2 %collective-permute-start = (bf16[4,128,128]{2,1,0:T(8,128)(2,1)S(1)}, bf16[4,128,128]{2,1,0:T(8,128)(2,1)S(1)}, u32[]{:S(2)}, u32[]{:S(2)}) collective-permute-start(bf16[4,128,128]{2,1,0:T(8,128)(2,1)S(1)} %copy.119), channel_id=1, source_target_pairs={{0,4},{4,8},{8,12},{12,16},{16,20},{20,24},{24,28},{28,32},{32,36}... | collective-permute-start | bytes 393224 | tf_op jit(solution)/shard_map/while/body/eval_jaxpr/ppermute | solution.py:15
  405.3 9.3 %collective-permute-start = (bf16[4,128,128]{2,1,0:T(8,128)(2,1)S(1)}, bf16[4,128,128]{2,1,0:T(8,128)(2,1)S(1)}, u32[]{:S(2)}, u32[]{:S(2)}) collective-permute-start(bf16[4,128,128]{2,1,0:T(8,128)(2,1)S(1)} %copy.119), channel_id=1, source_target_pairs={{0,4},{4,8},{8,12},{12,16},{16,20},{20,24},{24,28},{28,32},{32,36}... | collective-permute-start | bytes 393224 | tf_op jit(solution)/shard_map/while/body/eval_jaxpr/ppermute | solution.py:15
  414.6 9.0 %collective-permute-start = (bf16[4,128,128]{2,1,0:T(8,128)(2,1)S(1)}, bf16[4,128,128]{2,1,0:T(8,128)(2,1)S(1)}, u32[]{:S(2)}, u32[]{:S(2)}) collective-permute-start(bf16[4,128,128]{2,1,0:T(8,128)(2,1)S(1)} %copy.119), channel_id=1, source_target_pairs={{0,4},{4,8},{8,12},{12,16},{16,20},{20,24},{24,28},{28,32},{32,36}... | collective-permute-start | bytes 393224 | tf_op jit(solution)/shard_map/while/body/eval_jaxpr/ppermute | solution.py:15
  472.4 8.8 %collective-permute-start = (bf16[4,128,128]{2,1,0:T(8,128)(2,1)S(1)}, bf16[4,128,128]{2,1,0:T(8,128)(2,1)S(1)}, u32[]{:S(2)}, u32[]{:S(2)}) collective-permute-start(bf16[4,128,128]{2,1,0:T(8,128)(2,1)S(1)} %copy.119), channel_id=1, source_target_pairs={{0,4},{4,8},{8,12},{12,16},{16,20},{20,24},{24,28},{28,32},{32,36}... | collective-permute-start | bytes 393224 | tf_op jit(solution)/shard_map/while/body/eval_jaxpr/ppermute | solution.py:15
  481.2 9.4 %collective-permute-start = (bf16[4,128,128]{2,1,0:T(8,128)(2,1)S(1)}, bf16[4,128,128]{2,1,0:T(8,128)(2,1)S(1)}, u32[]{:S(2)}, u32[]{:S(2)}) collective-permute-start(bf16[4,128,128]{2,1,0:T(8,128)(2,1)S(1)} %copy.119), channel_id=1, source_target_pairs={{0,4},{4,8},{8,12},{12,16},{16,20},{20,24},{24,28},{28,32},{32,36}... | collective-permute-start | bytes 393224 | tf_op jit(solution)/shard_map/while/body/eval_jaxpr/ppermute | solution.py:15
  490.6 8.5 %collective-permute-start = (bf16[4,128,128]{2,1,0:T(8,128)(2,1)S(1)}, bf16[4,128,128]{2,1,0:T(8,128)(2,1)S(1)}, u32[]{:S(2)}, u32[]{:S(2)}) collective-permute-start(bf16[4,128,128]{2,1,0:T(8,128)(2,1)S(1)} %copy.119), channel_id=1, source_target_pairs={{0,4},{4,8},{8,12},{12,16},{16,20},{20,24},{24,28},{28,32},{32,36}... | collective-permute-start | bytes 393224 | tf_op jit(solution)/shard_map/while/body/eval_jaxpr/ppermute | solution.py:15
  539.8 8.2 %collective-permute-start = (bf16[4,128,128]{2,1,0:T(8,128)(2,1)S(1)}, bf16[4,128,128]{2,1,0:T(8,128)(2,1)S(1)}, u32[]{:S(2)}, u32[]{:S(2)}) collective-permute-start(bf16[4,128,128]{2,1,0:T(8,128)(2,1)S(1)} %copy.119), channel_id=1, source_target_pairs={{0,4},{4,8},{8,12},{12,16},{16,20},{20,24},{24,28},{28,32},{32,36}... | collective-permute-start | bytes 393224 | tf_op jit(solution)/shard_map/while/body/eval_jaxpr/ppermute | solution.py:15
  547.9 9.3 %collective-permute-start = (bf16[4,128,128]{2,1,0:T(8,128)(2,1)S(1)}, bf16[4,128,128]{2,1,0:T(8,128)(2,1)S(1)}, u32[]{:S(2)}, u32[]{:S(2)}) collective-permute-start(bf16[4,128,128]{2,1,0:T(8,128)(2,1)S(1)} %copy.119), channel_id=1, source_target_pairs={{0,4},{4,8},{8,12},{12,16},{16,20},{20,24},{24,28},{28,32},{32,36}... | collective-permute-start | bytes 393224 | tf_op jit(solution)/shard_map/while/body/eval_jaxpr/ppermute | solution.py:15
  557.3 9.0 %collective-permute-start = (bf16[4,128,128]{2,1,0:T(8,128)(2,1)S(1)}, bf16[4,128,128]{2,1,0:T(8,128)(2,1)S(1)}, u32[]{:S(2)}, u32[]{:S(2)}) collective-permute-start(bf16[4,128,128]{2,1,0:T(8,128)(2,1)S(1)} %copy.119), channel_id=1, source_target_pairs={{0,4},{4,8},{8,12},{12,16},{16,20},{20,24},{24,28},{28,32},{32,36}... | collective-permute-start | bytes 393224 | tf_op jit(solution)/shard_map/while/body/eval_jaxpr/ppermute | solution.py:15
  592.9 78.0 %all-to-all-start.6 = ((bf16[4,32,512]{2,1,0:T(8,128)(2,1)}), bf16[4,32,512]{2,1,0:T(8,128)(2,1)S(1)}, u32[]{:S(2)}, u32[]{:S(2)}) async-start(bf16[4,32,512]{2,1,0:T(8,128)(2,1)} %all_to_all.118), calls=%async_computation.6 | async-start | bytes 262144 | tf_op jit(solution)/shard_map/all_to_all | solution.py:113
  670.9 9.4 %all-to-all-start.7 = ((bf16[4,32,512]{2,1,0:T(8,128)(2,1)}), bf16[4,32,512]{2,1,0:T(8,128)(2,1)S(1)}, u32[]{:S(2)}, u32[]{:S(2)}) async-start(bf16[4,32,512]{2,1,0:T(8,128)(2,1)} %all_to_all.122), calls=%async_computation.7 | async-start | bytes 262144 | tf_op jit(solution)/shard_map/all_to_all | solution.py:114
  (31 other events, 210.5 us)
where the time goes:
time: 682 us; the launch traced here: 681 us
  waiting for transfers between devices  289 us (42%)
  local copies, waits for them, and re-layouts  169 us (25%)
  starting transfers between devices  110 us (16%)
  matrix products  87.5 us (13%)
  other arithmetic  14.9 us (2%)
  loops' own time  9.27 us (1%)
    ppermute x63, waiting for transfers between devices, passed_along(): return lax.ppermute(value, axis, pairs)  259 us
    gather x65, local copies, waits for them, and re-layouts, positions(): return (placed * BLK + local % BLK, jnp.take(block_docs, placed))  79.7 us
    gather x65, local copies, waits for them, and re-layouts, positions(): placed = jnp.take(block_plan, shard * blocks_per + local // BLK)  79.7 us
    all_to_all x1, starting transfers between devices, on_device(): lax.all_to_all(output_b, 'head', split_axis=0, concat_axis=1, tiled=True)  72.9 us
    dot_general x64, matrix products, absorb_masked(): jnp.einsum('hgqk,khd->qhgd', weight_b, valb, preferred_element_type=jnp.f...  17.8 us
    dot_general x64, matrix products, absorb_masked(): jnp.einsum('hgqk,khd->qhgd', wds_b, valb, preferred_element_type=jnp.floa...  15.7 us
    dot_general x64, matrix products, absorb_masked(): jnp.einsum('qhgd,khd->hgqk', query4, ktanb, preferred_element_type=jnp.fl...  14.5 us
    dot_general x64, matrix products, absorb_masked(): jnp.einsum('hgqk,khd->qhgd', weight_b, vtanb, preferred_element_type=jnp....  14.5 us
  transfers between devices with their start and end apart: 71, of which 70 were waited for; matrix products, arithmetic and copies ran while one was open for 39% of the time, Pallas kernels for 0%

commit v1 on v0

v1 whole, which is shorter than its diff:
```python
import functools
import math

import jax
import jax.numpy as jnp
from jax import lax
from jax.experimental import pallas as pl
from jax.experimental.pallas import tpu as pltpu
from jax.sharding import PartitionSpec as P

HD = 128
BLK = 128
SHARDS = 64
PIECES = 16
WINDOW = 8
NEG = -1e30
SCALE = 1.0 / math.sqrt(HD)
LOG2E = math.log2(math.e)
BF = jnp.bfloat16
F32 = jnp.float32
VMEM = pl.BlockSpec(memory_space=pltpu.VMEM)
SMEM = pl.BlockSpec(memory_space=pltpu.SMEM)


def lanes(start, size):
    return pl.ds(pl.multiple_of(start, 128), size)


def pack_keys(k, v, dk, dv, keep, send):
    core = lax.axis_index("head") % 2
    for y in range(2):
        for a, ref in enumerate((k, v, dk, dv)):
            keep[y, a] = ref[:, lanes((2 * y + core) * HD, HD)]
            send[y, a] = ref[:, lanes((2 * y + 1 - core) * HD, HD)]


def pack_queries(q, dq, own, to1, to2, to3):
    h = lax.axis_index("head")
    for j, out in enumerate((own, to1, to2, to3)):
        at = lanes(lax.bitwise_xor(h, j) * 512, 512)
        out[0] = q[:, at]
        out[1] = dq[:, at]


def spread(keep, got, out):
    core = lax.axis_index("head") % 2
    for y in range(2):
        for a in range(4):
            for r in range(4):
                rows = pl.ds(16 * (r % 2), 16)
                mine, other = keep[y, a, rows], got[y, a, rows]
                piece = jnp.where(core == r // 2, mine, other)
                for group in range(SHARDS // PIECES):
                    out[group * PIECES + a * 4 + r, y] = piece


def select(plan, docs, pieces, out, inverse):
    @pl.loop(0, SHARDS)
    def _(i):
        inverse[plan[i]] = i

    group = lax.axis_index("ctx") // PIECES
    for d in range(PIECES):
        t = plan[group * PIECES + d]
        for s in range(WINDOW):
            if s == 0:
                source = group * PIECES + d
            else:
                back = jnp.maximum(t - s, 0)
                same = jnp.logical_and(t >= s, docs[back] == docs[t])
                source = inverse[jnp.where(same, back, t)]
            out[d, s] = pieces[source]


def attend(plan, docs, q0, q1, q2, q3, keys, o0, o1, o2, o3):
    h = lax.axis_index("head")
    t = plan[lax.axis_index("ctx")]
    doc = docs[t]

    def gathered(a):
        return jnp.concatenate(
            [keys[a * 4 + r, s, y] for s in range(WINDOW) for y in range(2) for r in range(4)], axis=0
        )

    kk, vv, dkk, dvv = (gathered(a) for a in range(4))
    kdk = jnp.concatenate([kk, dkk], axis=1)
    vdv = jnp.concatenate([vv, dvv], axis=1)
    seen = []
    for s in range(1, WINDOW):
        back = jnp.maximum(t - s, 0)
        seen.append(jnp.logical_and(t >= s, docs[back] == doc))
    contract_last = (((1,), (1,)), ((), ()))
    for j, (q, o) in enumerate(((q0, o0), (q1, o1), (q2, o2), (q3, o3))):
        qa = jnp.concatenate([q[0, :, g * HD : (g + 1) * HD] for g in range(4)], axis=0)
        dqa = jnp.concatenate([q[1, :, g * HD : (g + 1) * HD] for g in range(4)], axis=0)
        score = lax.dot_general(qa, kk, contract_last, preferred_element_type=F32)
        dscore = lax.dot_general(
            jnp.concatenate([dqa, qa], axis=1), kdk, contract_last, preferred_element_type=F32
        )
        row = lax.broadcasted_iota(jnp.int32, (128, 128), 0) % 32 + 32 * lax.bitwise_xor(h, j)
        col = lax.broadcasted_iota(jnp.int32, (128, 128), 1)
        parts = [jnp.where(col <= row, score[:, :BLK], NEG)]
        for s in range(1, WINDOW):
            parts.append(jnp.where(seen[s - 1], score[:, s * BLK : (s + 1) * BLK], NEG))
        masked = jnp.concatenate(parts, axis=1)
        top = jnp.max(masked, axis=1, keepdims=True)
        weight = jnp.exp2((masked - top) * (SCALE * LOG2E))
        total = jnp.sum(weight, axis=1, keepdims=True)
        wds = weight * dscore
        curve = jnp.sum(wds, axis=1, keepdims=True) * SCALE
        ab = jnp.dot(weight.astype(BF), vdv, preferred_element_type=F32)
        b1 = jnp.dot(wds.astype(BF), vv, preferred_element_type=F32)
        inv = 1.0 / total
        a = ab[:, :HD] * inv
        b = (b1 * SCALE + ab[:, HD:]) * inv - (curve * inv) * a
        ab_, bb_ = a.astype(BF), b.astype(BF)
        for g in range(4):
            o[0, :, g * HD : (g + 1) * HD] = ab_[g * 32 : (g + 1) * 32]
            o[1, :, g * HD : (g + 1) * HD] = bb_[g * 32 : (g + 1) * 32]


def place(r0, r1, r2, r3, att, tan):
    h = lax.axis_index("head")
    for j, r in enumerate((r0, r1, r2, r3)):
        at = lanes(lax.bitwise_xor(h, j) * 512, 512)
        att[:, at] = r[0]
        tan[:, at] = r[1]


def struct(*shape):
    return jax.ShapeDtypeStruct(shape, BF)


def to_head(value, j):
    return lax.ppermute(value, "head", [(i, i ^ j) for i in range(4)])


def on_device(queries, key_rows, value_rows, query_tangent, key_tangent, value_tangent, plan, docs):
    keep, send = pl.pallas_call(
        pack_keys, out_shape=(struct(2, 4, 32, 128),) * 2, in_specs=[VMEM] * 4, out_specs=(VMEM,) * 2, name="pack_keys"
    )(key_rows, value_rows, key_tangent, value_tangent)
    got = to_head(send, 1)
    pieces = pl.pallas_call(
        spread, out_shape=struct(SHARDS, 2, 16, 128), in_specs=[VMEM] * 2, out_specs=VMEM, name="spread"
    )(keep, got)
    by_y = [[c * 4 + 2 * y + core for c in range(SHARDS) for y in range(2)] for core in range(2)]
    pieces = lax.all_to_all(
        pieces.reshape(SHARDS * 2, 16, 128), ("ctx", "head"), 0, 0, tiled=True, axis_index_groups=by_y
    ).reshape(SHARDS, 2, 16, 128)
    qs = pl.pallas_call(
        pack_queries, out_shape=(struct(2, 32, 512),) * 4, in_specs=[VMEM] * 2, out_specs=(VMEM,) * 4, name="pack_queries"
    )(queries, query_tangent)
    qs = [qs[0]] + [to_head(qs[j], j) for j in (1, 2, 3)]
    chosen = pl.pallas_call(
        select,
        out_shape=struct(PIECES, WINDOW, 2, 16, 128),
        in_specs=[SMEM, SMEM, VMEM],
        out_specs=VMEM,
        scratch_shapes=[pltpu.SMEM((SHARDS,), jnp.int32)],
        name="select",
    )(plan, docs, pieces)
    groups = [[g * PIECES + i for i in range(PIECES)] for g in range(SHARDS // PIECES)]
    chosen = lax.all_to_all(
        chosen.reshape(PIECES, WINDOW * 32, 128), "ctx", 0, 0, tiled=True, axis_index_groups=groups
    ).reshape(PIECES, WINDOW, 2, 16, 128)
    outs = pl.pallas_call(
        attend,
        out_shape=(struct(2, 32, 512),) * 4,
        in_specs=[SMEM, SMEM] + [VMEM] * 5,
        out_specs=(VMEM,) * 4,
        name="attend",
        compiler_params=pltpu.CompilerParams(vmem_limit_bytes=48 << 20),
    )(plan, docs, *qs, chosen)
    outs = [outs[0]] + [to_head(outs[j], j) for j in (1, 2, 3)]
    return pl.pallas_call(
        place, out_shape=(struct(32, 2048),) * 2, in_specs=[VMEM] * 4, out_specs=(VMEM,) * 2, name="place"
    )(*outs)


def solution(mesh):
    rows = P(("ctx", "head"), None)
    return jax.shard_map(
        on_device,
        mesh=mesh,
        in_specs=(rows,) * 6 + (P(), P()),
        out_specs=(rows, rows),
        check_vma=False,
    )
```

time: 682 us -> 82 us (0.12)
  waiting for transfers between devices: 289 us -> 17 us
  local copies, waits for them, and re-layouts: 169 us -> 3.38 us
  starting transfers between devices: 110 us -> 16.7 us
  matrix products: 87.5 us -> 0 us
  blocking collectives: 0 us -> 31.5 us
  other arithmetic: 14.9 us -> 0 us
  Pallas kernels: 0 us -> 12.2 us
  loops' own time: 9.27 us -> 0 us
    ppermute x63 -> x7, waiting for transfers between devices: 259 us -> 17 us  [to_head(): return lax.ppermute(value, 'head', [(i, i ^ j) for i in range(4)])]
    gather x130 -> x0, local copies, waits for them, and re-layouts: 159 us -> none  [the longest x65 79.7 us: positions(): return (placed * BLK + local % BLK, jnp.take(block_docs, placed))]
    all_to_all x8 -> x1, starting transfers between devices: 105 us -> 4.14 us  [on_device(): lax.all_to_all(chosen.reshape(PIECES, WINDOW * 32, 128), 'ctx', 0, 0, til...]
    dot_general x384 -> x0, matrix products: 87.5 us -> none  [the longest x64 17.8 us: absorb_masked(): jnp.einsum('hgqk,khd->qhgd', weight_b, valb, preferred_element_type=jnp.f...]
    all_to_all x0 -> x1, blocking collectives: none -> 31.5 us  [on_device(): lax.all_to_all(pieces.reshape(SHARDS * 2, 16, 128), ('ctx', 'head'), 0, 0...]
    all_to_all x8 -> x1, waiting for transfers between devices: 29.7 us -> 0.01 us  [on_device(): lax.all_to_all(chosen.reshape(PIECES, WINDOW * 32, 128), 'ctx', 0, 0, til...]
    pallas_call x0 -> x6, Pallas kernels: none -> 12.2 us  [the longest x1 3.04 us: on_device(): pl.pallas_call(select, out_shape=struct(PIECES, WINDOW, 2, 16, 128), in_s...]
    another operation x1 -> x0, loops' own time: 9.27 us -> none  [on_device(): state, stacked = lax.fori_loop(0, shards - 1, one_turn, (state, stacked))]
  transfers between devices with their start and end apart: 71 -> 8, of which waited for: 70 -> 5; matrix products, arithmetic and copies ran while one was open for 39% -> 0% of each run, Pallas kernels for 0% -> 2%
where the time goes in v1:
time: 82 us; the launch traced here: 81.5 us
  blocking collectives  31.5 us (38%)
  waiting for transfers between devices  17 us (21%)
  starting transfers between devices  16.7 us (20%)
  Pallas kernels  12.2 us (15%)
  local copies, waits for them, and re-layouts  3.38 us (4%)
    all_to_all x1, blocking collectives, on_device(): lax.all_to_all(pieces.reshape(SHARDS * 2, 16, 128), ('ctx', 'head'), 0, 0...  31.5 us
    ppermute x7, waiting for transfers between devices, to_head(): return lax.ppermute(value, 'head', [(i, i ^ j) for i in range(4)])  17 us
    ppermute x7, starting transfers between devices, to_head(): return lax.ppermute(value, 'head', [(i, i ^ j) for i in range(4)])  12.6 us
    all_to_all x1, starting transfers between devices, on_device(): lax.all_to_all(chosen.reshape(PIECES, WINDOW * 32, 128), 'ctx', 0, 0, til...  4.14 us
    unnamed x16, local copies, waits for them, and re-layouts  3.38 us
    pallas_call x1, Pallas kernels, on_device(): pl.pallas_call(select, out_shape=struct(PIECES, WINDOW, 2, 16, 128), in_s...  3.04 us
    pallas_call x1, Pallas kernels, on_device(): pl.pallas_call(attend, out_shape=(struct(2, 32, 512),) * 4, in_specs=[SME...  2.63 us
    pallas_call x1, Pallas kernels, on_device(): pl.pallas_call(spread, out_shape=struct(SHARDS, 2, 16, 128), in_specs=[VM...  1.75 us
  transfers between devices with their start and end apart: 8, of which 5 were waited for; matrix products, arithmetic and copies ran while one was open for 0% of the time, Pallas kernels for 2%

profile of v1, /device:TPU:1, one launch (start us, length us, event | category | flops | bytes accessed | tf_op | source)
XLA Modules:
  0.0 81.5 jit_solution(4103333038998993268)
XLA Ops:
  0.6 1.5 %pack_keys.1 = (bf16[2,4,32,128]{3,2,1,0:T(8,128)(2,1)}, bf16[2,4,32,128]{3,2,1,0:T(8,128)(2,1)}) custom-call(bf16[32,512]{1,0:T(8,128)(2,1)} %k.1, bf16[32,512]{1,0:T(8,128)(2,1)} %v.1, bf16[32,512]{1,0:T(8,128)(2,1)} %dk.1, bf16[32,512]{1,0:T(8,128)(2,1)} %dv.1), custom_call_target="tpu_custom_call" | custom-call | tf_op jit(solution)/shard_map/pack_keys/pallas_call | solution.py:139
  2.1 3.2 %collective-permute-start.3 = (bf16[2,4,32,128]{3,2,1,0:T(8,128)(2,1)}, bf16[2,4,32,128]{3,2,1,0:T(8,128)(2,1)S(1)}, u32[]{:S(2)}, u32[]{:S(2)}) collective-permute-start(bf16[2,4,32,128]{3,2,1,0:T(8,128)(2,1)} %get-tuple-element.17), channel_id=1, source_target_pairs={{0,1},{1,0},{2,3},{3,2},{4,5},{5,4},{6,7},{7,6},{8,9},{9,8},{10,11... | collective-permute-start | bytes 196616 | tf_op jit(solution)/shard_map/ppermute | solution.py:135
  5.4 1.1 %collective-permute-done.3.got = bf16[2,4,32,128]{3,2,1,0:T(8,128)(2,1)S(1)} collective-permute-done((bf16[2,4,32,128]{3,2,1,0:T(8,128)(2,1)}, bf16[2,4,32,128]{3,2,1,0:T(8,128)(2,1)S(1)}, u32[]{:S(2)}, u32[]{:S(2)}) %collective-permute-start.3) | collective-permute-done | bytes 65568 | tf_op jit(solution)/shard_map/ppermute | solution.py:135
  6.5 0.0 copy-start.4
  6.5 0.6 copy-done.4
  7.1 1.7 %spread.1 = bf16[64,2,16,128]{3,2,1,0:T(8,128)(2,1)} custom-call(bf16[2,4,32,128]{3,2,1,0:T(8,128)(2,1)} %get-tuple-element.16.keep, bf16[2,4,32,128]{3,2,1,0:T(8,128)(2,1)} %copy-done.4), custom_call_target="tpu_custom_call" | custom-call | tf_op jit(solution)/shard_map/spread/pallas_call | solution.py:143
  8.8 31.5 %all_to_all.10 = bf16[128,16,128]{2,1,0:T(8,128)(2,1)} all-to-all(bf16[128,16,128]{2,1,0:T(8,128)(2,1)} %bitcast.6), channel_id=1, replica_groups={{0,2,4,6,8,10,12,14,16,18,20,22,24,26,28,30,32,34,36,38,40,42,44,46,48,..., dimensions={0} | all-to-all | bytes 1048576 | tf_op jit(solution)/shard_map/all_to_all | solution.py:147
  40.3 3.0 %select.1 = bf16[16,8,2,16,128]{4,3,2,1,0:T(8,128)(2,1)} custom-call(s32[64]{0:T(128)} %plan.3, s32[64]{0:T(128)} %docs.3, bf16[64,2,16,128]{3,2,1,0:T(8,128)(2,1)} %bitcast.7), custom_call_target="tpu_custom_call" | custom-call | tf_op jit(solution)/shard_map/select/pallas_call | solution.py:154
  43.4 4.1 %all-to-all-start.1 = ((bf16[16,256,128]{2,1,0:T(8,128)(2,1)}), bf16[16,256,128]{2,1,0:T(8,128)(2,1)S(1)}, u32[]{:S(2)}, u32[]{:S(2)}) async-start(bf16[16,256,128]{2,1,0:T(8,128)(2,1)} %bitcast.5), calls=%async_computation.1 | async-start | bytes 2097152 | tf_op jit(solution)/shard_map/all_to_all | solution.py:163
  47.5 1.7 %pack_queries.1 = (bf16[2,32,512]{2,1,0:T(8,128)(2,1)}, bf16[2,32,512]{2,1,0:T(8,128)(2,1)}, bf16[2,32,512]{2,1,0:T(8,128)(2,1)}, bf16[2,32,512]{2,1,0:T(8,128)(2,1)}) custom-call(bf16[32,2048]{1,0:T(8,128)(2,1)} %q.1, bf16[32,2048]{1,0:T(8,128)(2,1)} %dq.1), custom_call_target="tpu_custom_call" | custom-call | tf_op jit(solution)/shard_map/pack_queries/pallas_call | solution.py:150
  49.2 2.5 %collective-permute-start = (bf16[2,32,512]{2,1,0:T(8,128)(2,1)}, bf16[2,32,512]{2,1,0:T(8,128)(2,1)S(1)}, u32[]{:S(2)}, u32[]{:S(2)}) collective-permute-start(bf16[2,32,512]{2,1,0:T(8,128)(2,1)} %get-tuple-element.13), channel_id=1, source_target_pairs={{0,1},{1,0},{2,3},{3,2},{4,5},{5,4},{6,7},{7,6},{8,9},{9,8},{10,11... | collective-permute-start | bytes 196616 | tf_op jit(solution)/shard_map/ppermute | solution.py:135
  51.7 1.9 %collective-permute-start.1 = (bf16[2,32,512]{2,1,0:T(8,128)(2,1)}, bf16[2,32,512]{2,1,0:T(8,128)(2,1)S(1)}, u32[]{:S(2)}, u32[]{:S(2)}) collective-permute-start(bf16[2,32,512]{2,1,0:T(8,128)(2,1)} %get-tuple-element.14), channel_id=1, source_target_pairs={{0,2},{1,3},{2,0},{3,1},{4,6},{5,7},{6,4},{7,5},{8,10},{9,11},{10,... | collective-permute-start | bytes 196616 | tf_op jit(solution)/shard_map/ppermute | solution.py:135
  53.6 1.3 %collective-permute-start.2 = (bf16[2,32,512]{2,1,0:T(8,128)(2,1)}, bf16[2,32,512]{2,1,0:T(8,128)(2,1)S(1)}, u32[]{:S(2)}, u32[]{:S(2)}) collective-permute-start(bf16[2,32,512]{2,1,0:T(8,128)(2,1)} %get-tuple-element.15), channel_id=1, source_target_pairs={{0,3},{1,2},{2,1},{3,0},{4,7},{5,6},{6,5},{7,4},{8,11},{9,10},{10,... | collective-permute-start | bytes 196616 | tf_op jit(solution)/shard_map/ppermute | solution.py:135
  54.9 0.0 collective-permute-done.q1
  54.9 10.7 %collective-permute-done.1.q2 = bf16[2,32,512]{2,1,0:T(8,128)(2,1)S(1)} collective-permute-done((bf16[2,32,512]{2,1,0:T(8,128)(2,1)}, bf16[2,32,512]{2,1,0:T(8,128)(2,1)S(1)}, u32[]{:S(2)}, u32[]{:S(2)}) %collective-permute-start.1) | collective-permute-done | bytes 65568 | tf_op jit(solution)/shard_map/ppermute | solution.py:135
  65.5 1.4 %collective-permute-done.2.q3 = bf16[2,32,512]{2,1,0:T(8,128)(2,1)S(1)} collective-permute-done((bf16[2,32,512]{2,1,0:T(8,128)(2,1)}, bf16[2,32,512]{2,1,0:T(8,128)(2,1)S(1)}, u32[]{:S(2)}, u32[]{:S(2)}) %collective-permute-start.2) | collective-permute-done | bytes 65568 | tf_op jit(solution)/shard_map/ppermute | solution.py:135
  66.9 0.0 all-to-all-done.1
  67.0 0.0 copy-start.2
  67.0 0.0 copy-start.3
  67.0 0.7 copy-done.2
  67.6 0.0 copy-done.3
  67.6 0.0 copy-start
  67.6 0.8 %copy-done = bf16[2,32,512]{2,1,0:T(8,128)(2,1)S(1)} copy-done((bf16[2,32,512]{2,1,0:T(8,128)(2,1)S(1)}, bf16[2,32,512]{2,1,0:T(8,128)(2,1)}, u32[]{:S(2)}) %copy-start) | copy-done | bytes 65560
  68.5 2.6 %attend.1 = (bf16[2,32,512]{2,1,0:T(8,128)(2,1)S(1)}, bf16[2,32,512]{2,1,0:T(8,128)(2,1)S(1)}, bf16[2,32,512]{2,1,0:T(8,128)(2,1)S(1)}, bf16[2,32,512]{2,1,0:T(8,128)(2,1)S(1)}) custom-call(s32[64]{0:T(128)S(1)} %copy-done.2, s32[64]{0:T(128)S(1)} %copy-done.3, bf16[2,32,512]{2,1,0:T(8,128)(2,1)S(1)} %copy-done, ...), custom_call_target="tpu_custom_call" | custom-call | tf_op jit(solution)/shard_map/attend/pallas_call | solution.py:166
  71.1 0.0 copy-start.1
  71.1 0.6 copy-done.1
  71.7 0.4 collective-permute-start.4
  72.1 1.5 %collective-permute-start.5 = (bf16[2,32,512]{2,1,0:T(8,128)(2,1)S(1)}, bf16[2,32,512]{2,1,0:T(8,128)(2,1)S(1)}, u32[]{:S(2)}, u32[]{:S(2)}) collective-permute-start(bf16[2,32,512]{2,1,0:T(8,128)(2,1)S(1)} %get-tuple-element.20), channel_id=1, source_target_pairs={{0,2},{1,3},{2,0},{3,1},{4,6},{5,7},{6,4},{7,5},{8,10},{9,11},{10,... | collective-permute-start | bytes 196616 | tf_op jit(solution)/shard_map/ppermute | solution.py:135
  73.6 1.7 %collective-permute-start.6 = (bf16[2,32,512]{2,1,0:T(8,128)(2,1)S(1)}, bf16[2,32,512]{2,1,0:T(8,128)(2,1)S(1)}, u32[]{:S(2)}, u32[]{:S(2)}) collective-permute-start(bf16[2,32,512]{2,1,0:T(8,128)(2,1)S(1)} %get-tuple-element.21), channel_id=1, source_target_pairs={{0,3},{1,2},{2,1},{3,0},{4,7},{5,6},{6,5},{7,4},{8,11},{9,10},{10,... | collective-permute-start | bytes 196616 | tf_op jit(solution)/shard_map/ppermute | solution.py:135
  75.4 0.0 collective-permute-done.4.r1
  75.4 0.0 copy-start.5
  75.4 1.9 %collective-permute-done.5.r2 = bf16[2,32,512]{2,1,0:T(8,128)(2,1)S(1)} collective-permute-done((bf16[2,32,512]{2,1,0:T(8,128)(2,1)S(1)}, bf16[2,32,512]{2,1,0:T(8,128)(2,1)S(1)}, u32[]{:S(2)}, u32[]{:S(2)}) %collective-permute-start.5) | collective-permute-done | bytes 65568 | tf_op jit(solution)/shard_map/ppermute | solution.py:135
  77.3 0.0 copy-start.6
  77.3 1.9 %collective-permute-done.6.r3 = bf16[2,32,512]{2,1,0:T(8,128)(2,1)S(1)} collective-permute-done((bf16[2,32,512]{2,1,0:T(8,128)(2,1)S(1)}, bf16[2,32,512]{2,1,0:T(8,128)(2,1)S(1)}, u32[]{:S(2)}, u32[]{:S(2)}) %collective-permute-start.6) | collective-permute-done | bytes 65568 | tf_op jit(solution)/shard_map/ppermute | solution.py:135
  79.2 0.0 copy-start.7
  79.2 0.0 copy-done.5
  79.2 0.0 copy-done.6
  79.2 0.6 copy-done.7
  79.8 1.7 %place.1 = (bf16[32,2048]{1,0:T(8,128)(2,1)}, bf16[32,2048]{1,0:T(8,128)(2,1)}) custom-call(bf16[2,32,512]{2,1,0:T(8,128)(2,1)} %copy-done.1, bf16[2,32,512]{2,1,0:T(8,128)(2,1)} %copy-done.5, bf16[2,32,512]{2,1,0:T(8,128)(2,1)} %copy-done.6, bf16[2,32,512]{2,1,0:T(8,128)(2,1)} %copy-done.7), custom_call_target="tpu_custom_call" | custom-call | tf_op jit(solution)/shard_map/place/pallas_call | solution.py:175
Async XLA Ops:
  2.1 4.4 %collective-permute-start.3 = (bf16[2,4,32,128]{3,2,1,0:T(8,128)(2,1)}, bf16[2,4,32,128]{3,2,1,0:T(8,128)(2,1)S(1)}, u32[]{:S(2)}, u32[]{:S(2)}) collective-permute-start(bf16[2,4,32,128]{3,2,1,0:T(8,128)(2,1)} %get-tuple-element.17), channel_id=1, source_target_pairs={{0,1},{1,0},{2,3},{3,2},{4,5},{5,4},{6,7},{7,6},{8,9},{9,8},{10,11... | collective-permute-start | bytes 196616 | tf_op jit(solution)/shard_map/ppermute | solution.py:135
  6.5 0.6 copy-start.4
  43.4 23.6 %all-to-all-start.1 = ((bf16[16,256,128]{2,1,0:T(8,128)(2,1)}), bf16[16,256,128]{2,1,0:T(8,128)(2,1)S(1)}, u32[]{:S(2)}, u32[]{:S(2)}) async-start(bf16[16,256,128]{2,1,0:T(8,128)(2,1)} %bitcast.5), calls=%async_computation.1 | async-start | bytes 2097152 | tf_op jit(solution)/shard_map/all_to_all | solution.py:163
  49.2 5.7 %collective-permute-start = (bf16[2,32,512]{2,1,0:T(8,128)(2,1)}, bf16[2,32,512]{2,1,0:T(8,128)(2,1)S(1)}, u32[]{:S(2)}, u32[]{:S(2)}) collective-permute-start(bf16[2,32,512]{2,1,0:T(8,128)(2,1)} %get-tuple-element.13), channel_id=1, source_target_pairs={{0,1},{1,0},{2,3},{3,2},{4,5},{5,4},{6,7},{7,6},{8,9},{9,8},{10,11... | collective-permute-start | bytes 196616 | tf_op jit(solution)/shard_map/ppermute | solution.py:135
  51.7 13.8 %collective-permute-start.1 = (bf16[2,32,512]{2,1,0:T(8,128)(2,1)}, bf16[2,32,512]{2,1,0:T(8,128)(2,1)S(1)}, u32[]{:S(2)}, u32[]{:S(2)}) collective-permute-start(bf16[2,32,512]{2,1,0:T(8,128)(2,1)} %get-tuple-element.14), channel_id=1, source_target_pairs={{0,2},{1,3},{2,0},{3,1},{4,6},{5,7},{6,4},{7,5},{8,10},{9,11},{10,... | collective-permute-start | bytes 196616 | tf_op jit(solution)/shard_map/ppermute | solution.py:135
  53.6 13.3 %collective-permute-start.2 = (bf16[2,32,512]{2,1,0:T(8,128)(2,1)}, bf16[2,32,512]{2,1,0:T(8,128)(2,1)S(1)}, u32[]{:S(2)}, u32[]{:S(2)}) collective-permute-start(bf16[2,32,512]{2,1,0:T(8,128)(2,1)} %get-tuple-element.15), channel_id=1, source_target_pairs={{0,3},{1,2},{2,1},{3,0},{4,7},{5,6},{6,5},{7,4},{8,11},{9,10},{10,... | collective-permute-start | bytes 196616 | tf_op jit(solution)/shard_map/ppermute | solution.py:135
  67.0 0.7 copy-start.2
  67.0 0.7 copy-start.3
  67.6 0.8 %copy-start = (bf16[2,32,512]{2,1,0:T(8,128)(2,1)S(1)}, bf16[2,32,512]{2,1,0:T(8,128)(2,1)}, u32[]{:S(2)}) copy-start(bf16[2,32,512]{2,1,0:T(8,128)(2,1)} %get-tuple-element.12.q0) | copy-start | bytes 196612
  71.1 0.6 copy-start.1
  71.7 3.6 %collective-permute-start.4 = (bf16[2,32,512]{2,1,0:T(8,128)(2,1)S(1)}, bf16[2,32,512]{2,1,0:T(8,128)(2,1)S(1)}, u32[]{:S(2)}, u32[]{:S(2)}) collective-permute-start(bf16[2,32,512]{2,1,0:T(8,128)(2,1)S(1)} %get-tuple-element.19), channel_id=1, source_target_pairs={{0,1},{1,0},{2,3},{3,2},{4,5},{5,4},{6,7},{7,6},{8,9},{9,8},{10,11... | collective-permute-start | bytes 196616 | tf_op jit(solution)/shard_map/ppermute | solution.py:135
  72.1 5.2 %collective-permute-start.5 = (bf16[2,32,512]{2,1,0:T(8,128)(2,1)S(1)}, bf16[2,32,512]{2,1,0:T(8,128)(2,1)S(1)}, u32[]{:S(2)}, u32[]{:S(2)}) collective-permute-start(bf16[2,32,512]{2,1,0:T(8,128)(2,1)S(1)} %get-tuple-element.20), channel_id=1, source_target_pairs={{0,2},{1,3},{2,0},{3,1},{4,6},{5,7},{6,4},{7,5},{8,10},{9,11},{10,... | collective-permute-start | bytes 196616 | tf_op jit(solution)/shard_map/ppermute | solution.py:135
  73.6 5.6 %collective-permute-start.6 = (bf16[2,32,512]{2,1,0:T(8,128)(2,1)S(1)}, bf16[2,32,512]{2,1,0:T(8,128)(2,1)S(1)}, u32[]{:S(2)}, u32[]{:S(2)}) collective-permute-start(bf16[2,32,512]{2,1,0:T(8,128)(2,1)S(1)} %get-tuple-element.21), channel_id=1, source_target_pairs={{0,3},{1,2},{2,1},{3,0},{4,7},{5,6},{6,5},{7,4},{8,11},{9,10},{10,... | collective-permute-start | bytes 196616 | tf_op jit(solution)/shard_map/ppermute | solution.py:135
  75.4 3.8 %copy-start.5 = (bf16[2,32,512]{2,1,0:T(8,128)(2,1)}, bf16[2,32,512]{2,1,0:T(8,128)(2,1)S(1)}, u32[]{:S(2)}) copy-start(bf16[2,32,512]{2,1,0:T(8,128)(2,1)S(1)} %collective-permute-done.4.r1) | copy-start | bytes 196612
  77.3 1.9 %copy-start.6 = (bf16[2,32,512]{2,1,0:T(8,128)(2,1)}, bf16[2,32,512]{2,1,0:T(8,128)(2,1)S(1)}, u32[]{:S(2)}) copy-start(bf16[2,32,512]{2,1,0:T(8,128)(2,1)S(1)} %collective-permute-done.5.r2) | copy-start | bytes 196612
  79.2 0.6 copy-start.7

commit v2 on v1

v2 whole, which is shorter than its diff:
```python
import functools
import math

import jax
import jax.numpy as jnp
from jax import lax
from jax.experimental import pallas as pl
from jax.experimental.pallas import tpu as pltpu
from jax.sharding import PartitionSpec as P

HD = 128
BLK = 128
SHARDS = 64
PIECES = 16
WINDOW = 8
NEG = -1e30
SCALE = 1.0 / math.sqrt(HD)
LOG2E = math.log2(math.e)
BF = jnp.bfloat16
F32 = jnp.float32
VMEM = pl.BlockSpec(memory_space=pltpu.VMEM)
HBM = pl.BlockSpec(memory_space=pltpu.HBM)
SMEM = pl.BlockSpec(memory_space=pltpu.SMEM)


def lanes(start, size):
    return pl.ds(pl.multiple_of(start, 128), size)


def fetch_all(copies):
    for copy in copies:
        copy.start()
    for copy in copies:
        copy.wait()


def pack_keys(k, v, dk, dv, send):
    other = 1 - lax.axis_index("head") % 2
    for y in range(2):
        for a, ref in enumerate((k, v, dk, dv)):
            send[y, a] = ref[:, lanes((2 * y + other) * HD, HD)]


def pack_queries(q, dq, own, near, far, sems):
    h = lax.axis_index("head")
    copies = []
    for j, out in enumerate((own, near, far.at[0], far.at[1])):
        for i, ref in enumerate((q, dq)):
            source = ref.at[:, lanes(lax.bitwise_xor(h, j) * 512, 512)]
            copies.append(pltpu.make_async_copy(source, out.at[i], sems.at[len(copies)]))
    fetch_all(copies)


def spread(k, v, dk, dv, got, out):
    core = lax.axis_index("head") % 2
    for y in range(2):
        for a, ref in enumerate((k, v, dk, dv)):
            own = ref[:, lanes((2 * y + core) * HD, HD)]
            for r in range(4):
                at = 16 * (r % 2)
                piece = jnp.where(core == r // 2, own[at : at + 16], got[y, a, at : at + 16])
                for group in range(SHARDS // PIECES):
                    out[group * PIECES + a * 4 + r, y] = piece


def plan_sources(plan, docs, table, inverse):
    @pl.loop(0, SHARDS)
    def _(i):
        inverse[plan[i]] = i

    shard = lax.axis_index("ctx")
    group = shard // PIECES

    def fill(first, t, flags):
        doc = docs[t]
        for s in range(WINDOW):
            back = jnp.maximum(t - s, 0)
            same = jnp.logical_and(t >= s, docs[back] == doc)
            table[first + s] = same.astype(jnp.int32) if flags else inverse[jnp.where(same, back, t)]

    @pl.loop(0, PIECES)
    def _(d):
        fill(d * WINDOW, plan[group * PIECES + d], False)

    fill(PIECES * WINDOW, plan[shard], True)


def select(table, pieces, out):
    for d in range(PIECES):
        for s in range(WINDOW):
            out[d, s] = pieces[table[d * WINDOW + s]]


def attend(groups, table, keys, q_refs, o_refs):
    h = lax.axis_index("head")

    def gathered(a):
        return jnp.concatenate(
            [keys[a * 4 + r, s, y] for s in range(WINDOW) for y in range(2) for r in range(4)], axis=0
        )

    kk, vv, dkk, dvv = (gathered(a) for a in range(4))
    kdk = jnp.concatenate([kk, dkk], axis=1)
    vdv = jnp.concatenate([vv, dvv], axis=1)
    seen = [table[PIECES * WINDOW + s] == 1 for s in range(1, WINDOW)]
    contract_last = (((1,), (1,)), ((), ()))
    for j, q, o in zip(groups, q_refs, o_refs):
        qa = jnp.concatenate([q[0, :, g * HD : (g + 1) * HD] for g in range(4)], axis=0)
        dqa = jnp.concatenate([q[1, :, g * HD : (g + 1) * HD] for g in range(4)], axis=0)
        score = lax.dot_general(qa, kk, contract_last, preferred_element_type=F32)
        dscore = lax.dot_general(
            jnp.concatenate([dqa, qa], axis=1), kdk, contract_last, preferred_element_type=F32
        )
        row = lax.broadcasted_iota(jnp.int32, (128, 128), 0) % 32 + 32 * lax.bitwise_xor(h, j)
        col = lax.broadcasted_iota(jnp.int32, (128, 128), 1)
        parts = [jnp.where(col <= row, score[:, :BLK], NEG)]
        for s in range(1, WINDOW):
            parts.append(jnp.where(seen[s - 1], score[:, s * BLK : (s + 1) * BLK], NEG))
        masked = jnp.concatenate(parts, axis=1)
        top = jnp.max(masked, axis=1, keepdims=True)
        weight = jnp.exp2((masked - top) * (SCALE * LOG2E))
        total = jnp.sum(weight, axis=1, keepdims=True)
        wds = weight * dscore
        curve = jnp.sum(wds, axis=1, keepdims=True) * SCALE
        ab = jnp.dot(weight.astype(BF), vdv, preferred_element_type=F32)
        b1 = jnp.dot(wds.astype(BF), vv, preferred_element_type=F32)
        inv = 1.0 / total
        a = ab[:, :HD] * inv
        b = (b1 * SCALE + ab[:, HD:]) * inv - (curve * inv) * a
        ab_, bb_ = a.astype(BF), b.astype(BF)
        for g in range(4):
            o[0, :, g * HD : (g + 1) * HD] = ab_[g * 32 : (g + 1) * 32]
            o[1, :, g * HD : (g + 1) * HD] = bb_[g * 32 : (g + 1) * 32]


def attend_far(table, keys, direct, passed, out):
    attend((2, 3), table, keys, (direct.at[0], passed.at[1]), (out.at[0], out.at[1]))


def attend_near(table, keys, own, near, out_own, out_near):
    attend((0, 1), table, keys, (own, near), (out_own, out_near))


def place(own, near, direct, passed, att, tan):
    h = lax.axis_index("head")
    for j, r in enumerate((own, near, direct.at[0], passed.at[1])):
        at = lanes(lax.bitwise_xor(h, j) * 512, 512)
        att[:, at] = r[0]
        tan[:, at] = r[1]


def struct(*shape):
    return jax.ShapeDtypeStruct(shape, BF)


def to_head(value, j):
    return lax.ppermute(value, "head", [(i, i ^ j) for i in range(4)])


def call(body, out, *args, smem=0, limit=4, scratch=(), out_smem=False, source=VMEM, target=VMEM, cost=None):
    many = isinstance(out, tuple)
    place = SMEM if out_smem else target
    return pl.pallas_call(
        body,
        out_shape=out,
        in_specs=[SMEM] * smem + [source] * (len(args) - smem),
        out_specs=(place,) * len(out) if many else place,
        scratch_shapes=scratch,
        compiler_params=pltpu.CompilerParams(vmem_limit_bytes=limit << 20),
        cost_estimate=cost,
        name=body.__name__,
    )(*args)


def on_device(queries, key_rows, value_rows, query_tangent, key_tangent, value_tangent, plan, docs):
    rows = (key_rows, value_rows, key_tangent, value_tangent)
    got = to_head(call(pack_keys, struct(2, 4, 32, 128), *rows, limit=60), 1)
    pieces = call(spread, struct(SHARDS, 2, 16, 128), *rows, got)
    by_y = [[c * 4 + 2 * y + core for c in range(SHARDS) for y in range(2)] for core in range(2)]
    pieces = lax.all_to_all(
        pieces.reshape(SHARDS * 2, 16, 128), ("ctx", "head"), 0, 0, tiled=True, axis_index_groups=by_y
    ).reshape(SHARDS, 2, 16, 128)
    table = call(
        plan_sources,
        jax.ShapeDtypeStruct((PIECES * WINDOW + WINDOW,), jnp.int32),
        plan,
        docs,
        smem=2,
        out_smem=True,
        scratch=[pltpu.SMEM((SHARDS,), jnp.int32)],
        cost=pl.CostEstimate(flops=2_000_000_000, transcendentals=0, bytes_accessed=1_000_000),
    )
    own, near, far = call(
        pack_queries,
        (struct(2, 32, 512), struct(2, 32, 512), struct(2, 2, 32, 512)),
        queries,
        query_tangent,
        source=HBM,
        scratch=[pltpu.SemaphoreType.DMA((8,))],
    )
    far = to_head(far, 2)
    near = to_head(near, 1)
    far, near, table = lax.optimization_barrier((far, near, table))
    passed = to_head(far, 1)
    pieces, table, own, near, far, passed = lax.optimization_barrier((pieces, table, own, near, far, passed))
    chosen = call(select, struct(PIECES, WINDOW, 2, 16, 128), table, pieces, smem=1)
    groups = [[g * PIECES + i for i in range(PIECES)] for g in range(SHARDS // PIECES)]
    chosen = lax.all_to_all(
        chosen.reshape(PIECES, WINDOW * 32, 128), "ctx", 0, 0, tiled=True, axis_index_groups=groups
    ).reshape(PIECES, WINDOW, 2, 16, 128)
    cost = pl.CostEstimate(flops=400_000_000, transcendentals=262_144, bytes_accessed=1_500_000)
    far = call(attend_far, struct(2, 2, 32, 512), table, chosen, far, passed, smem=1, limit=24, cost=cost)
    chosen, own, near, far = lax.optimization_barrier((chosen, own, near, far))
    far = to_head(far, 2)
    own, near = call(attend_near, (struct(2, 32, 512),) * 2, table, chosen, own, near, smem=1, limit=24, cost=cost)
    near = to_head(near, 1)
    far, own, near = lax.optimization_barrier((far, own, near))
    passed = to_head(far, 1)
    return call(place, (struct(32, 2048),) * 2, own, near, far, passed)


def solution(mesh):
    rows = P(("ctx", "head"), None)
    return jax.shard_map(
        on_device,
        mesh=mesh,
        in_specs=(rows,) * 6 + (P(), P()),
        out_specs=(rows, rows),
        check_vma=False,
    )
```

time: 82 us -> 70.5 us (0.86)
  blocking collectives: 31.5 us -> 17.5 us
  starting transfers between devices: 16.7 us -> 28.4 us
  local copies, waits for them, and re-layouts: 3.38 us -> 0.04 us
  waiting for transfers between devices: 17 us -> 14 us
  Pallas kernels: 12.2 us -> 9.59 us
    all_to_all x1, blocking collectives: 31.5 us -> 17.5 us  [on_device(): lax.all_to_all(chosen.reshape(PIECES, WINDOW * 32, 128), 'ctx', 0, 0, til...]
    all_to_all x1, starting transfers between devices: 4.14 us -> 13.9 us  [on_device(): lax.all_to_all(pieces.reshape(SHARDS * 2, 16, 128), ('ctx', 'head'), 0, 0...]
    ppermute x7, waiting for transfers between devices: 17 us -> 7.96 us  [to_head(): return lax.ppermute(value, 'head', [(i, i ^ j) for i in range(4)])]
    all_to_all x1, waiting for transfers between devices: 0.01 us -> 6.04 us  [on_device(): lax.all_to_all(pieces.reshape(SHARDS * 2, 16, 128), ('ctx', 'head'), 0, 0...]
    unnamed x16, local copies, waits for them, and re-layouts: 3.38 us -> 0.04 us
    pallas_call x6 -> x8, Pallas kernels: 12.2 us -> 9.59 us  [call(): pl.pallas_call(body, out_shape=out, in_specs=[SMEM] * smem + [source] * (...]
    ppermute x7, starting transfers between devices: 12.6 us -> 14.5 us  [to_head(): return lax.ppermute(value, 'head', [(i, i ^ j) for i in range(4)])]
  transfers between devices with their start and end apart: 8 -> 8, of which waited for: 5 -> 6; matrix products, arithmetic and copies ran while one was open for 0% -> 0% of each run, Pallas kernels for 2% -> 6%
where the time goes in v2:
time: 70.5 us; the launch traced here: 70.3 us
  starting transfers between devices  28.4 us (40%)
  blocking collectives  17.5 us (25%)
  waiting for transfers between devices  14 us (20%)
  Pallas kernels  9.59 us (14%)
  between operations  0.76 us (1%)
    all_to_all x1, blocking collectives, on_device(): lax.all_to_all(chosen.reshape(PIECES, WINDOW * 32, 128), 'ctx', 0, 0, til...  17.5 us
    ppermute x7, starting transfers between devices, to_head(): return lax.ppermute(value, 'head', [(i, i ^ j) for i in range(4)])  14.5 us
    all_to_all x1, starting transfers between devices, on_device(): lax.all_to_all(pieces.reshape(SHARDS * 2, 16, 128), ('ctx', 'head'), 0, 0...  13.9 us
    pallas_call x8, Pallas kernels, call(): pl.pallas_call(body, out_shape=out, in_specs=[SMEM] * smem + [source] * (...  9.59 us
    ppermute x7, waiting for transfers between devices, to_head(): return lax.ppermute(value, 'head', [(i, i ^ j) for i in range(4)])  7.96 us
    all_to_all x1, waiting for transfers between devices, on_device(): lax.all_to_all(pieces.reshape(SHARDS * 2, 16, 128), ('ctx', 'head'), 0, 0...  6.04 us
  transfers between devices with their start and end apart: 8, of which 6 were waited for; matrix products, arithmetic and copies ran while one was open for 0% of the time, Pallas kernels for 6%

profile of v2, /device:TPU:1, one launch (start us, length us, event | category | flops | bytes accessed | tf_op | source)
XLA Modules:
  0.0 70.3 jit_solution(16048014383247192624)
XLA Ops:
  0.6 0.0 copy-start.5
  0.6 0.0 copy-start.4
  0.7 0.0 copy-start.3
  0.7 0.0 copy-start.2
  0.7 1.5 %pack_keys.1 = bf16[2,4,32,128]{3,2,1,0:T(8,128)(2,1)} custom-call(bf16[32,512]{1,0:T(8,128)(2,1)} %k.3, bf16[32,512]{1,0:T(8,128)(2,1)} %v.3, bf16[32,512]{1,0:T(8,128)(2,1)} %dk.3, bf16[32,512]{1,0:T(8,128)(2,1)} %dv.3), custom_call_target="tpu_custom_call" | custom-call | tf_op jit(solution)/shard_map/pack_keys/pallas_call | solution.py:163
  2.1 3.2 %collective-permute-start = (bf16[2,4,32,128]{3,2,1,0:T(8,128)(2,1)}, bf16[2,4,32,128]{3,2,1,0:T(8,128)(2,1)S(1)}, u32[]{:S(2)}, u32[]{:S(2)}) collective-permute-start(bf16[2,4,32,128]{3,2,1,0:T(8,128)(2,1)} %pack_keys.1), channel_id=1, source_target_pairs={{0,1},{1,0},{2,3},{3,2},{4,5},{5,4},{6,7},{7,6},{8,9},{9,8},{10,11... | collective-permute-start | bytes 196616 | tf_op jit(solution)/shard_map/ppermute | solution.py:157
  5.4 1.1 %collective-permute-done.got = bf16[2,4,32,128]{3,2,1,0:T(8,128)(2,1)S(1)} collective-permute-done((bf16[2,4,32,128]{3,2,1,0:T(8,128)(2,1)}, bf16[2,4,32,128]{3,2,1,0:T(8,128)(2,1)S(1)}, u32[]{:S(2)}, u32[]{:S(2)}) %collective-permute-start) | collective-permute-done | bytes 65568 | tf_op jit(solution)/shard_map/ppermute | solution.py:157
  6.5 0.0 copy-done.5
  6.5 0.0 copy-done.4
  6.5 0.0 copy-done.3
  6.5 0.0 copy-done.2
  6.5 0.9 %spread.1 = bf16[64,2,16,128]{3,2,1,0:T(8,128)(2,1)} custom-call(bf16[32,512]{1,0:T(8,128)(2,1)S(1)} %copy-done.2, bf16[32,512]{1,0:T(8,128)(2,1)S(1)} %copy-done.3, bf16[32,512]{1,0:T(8,128)(2,1)S(1)} %copy-done.4, bf16[32,512]{1,0:T(8,128)(2,1)S(1)} %copy-done.5, bf16[2,4,32,128]{3,2,1,0:T(8,128)(2,1)S(1)} %collective-permute-done.got), custom_call_target="tpu_custom_call" | custom-call | tf_op jit(solution)/shard_map/spread/pallas_call | solution.py:163
  7.4 0.0 copy-start
  7.4 0.0 copy-start.1
  7.4 13.9 %all-to-all-start = ((bf16[128,16,128]{2,1,0:T(8,128)(2,1)}), bf16[128,16,128]{2,1,0:T(8,128)(2,1)S(1)}, u32[]{:S(2)}, u32[]{:S(2)}) async-start(bf16[128,16,128]{2,1,0:T(8,128)(2,1)} %bitcast), calls=%async_computation | async-start | bytes 1048576 | tf_op jit(solution)/shard_map/all_to_all | solution.py:180
  21.3 0.0 copy-done
  21.3 0.0 copy-done.1
  21.3 0.2 pack_queries.1
  21.5 0.0 copy-start.6
  21.5 0.0 copy-start.7
  21.6 0.7 %collective-permute-start.2 = (bf16[2,32,512]{2,1,0:T(8,128)(2,1)S(1)}, bf16[2,32,512]{2,1,0:T(8,128)(2,1)S(1)}, u32[]{:S(2)}, u32[]{:S(2)}) collective-permute-start(bf16[2,32,512]{2,1,0:T(8,128)(2,1)S(1)} %get-tuple-element.24), channel_id=1, source_target_pairs={{0,1},{1,0},{2,3},{3,2},{4,5},{5,4},{6,7},{7,6},{8,9},{9,8},{10,11... | collective-permute-start | bytes 196616 | tf_op jit(solution)/shard_map/ppermute | solution.py:157
  22.3 2.4 %collective-permute-start.1 = (bf16[2,2,32,512]{3,2,1,0:T(8,128)(2,1)S(1)}, bf16[2,2,32,512]{3,2,1,0:T(8,128)(2,1)S(1)}, u32[]{:S(2)}, u32[]{:S(2)}) collective-permute-start(bf16[2,2,32,512]{3,2,1,0:T(8,128)(2,1)S(1)} %get-tuple-element.23), channel_id=1, source_target_pairs={{0,2},{1,3},{2,0},{3,1},{4,6},{5,7},{6,4},{7,5},{8,10},{9,11},{10,... | collective-permute-start | bytes 393224 | tf_op jit(solution)/shard_map/ppermute | solution.py:157
  24.7 0.0 copy-done.6
  24.7 0.0 copy-done.7
  24.7 2.3 %plan_sources.1.table = s32[136]{0:T(256)S(1)} custom-call(s32[64]{0:T(128)S(1)} %copy-done.6, s32[64]{0:T(128)S(1)} %copy-done.7), custom_call_target="tpu_custom_call" | custom-call | flops 2000000000 | bytes 1000000 | tf_op jit(solution)/shard_map/plan_sources/pallas_call | solution.py:163
  27.0 0.0 collective-permute-done.2.near
  27.0 4.0 %collective-permute-done.1.direct = bf16[2,2,32,512]{3,2,1,0:T(8,128)(2,1)S(1)} collective-permute-done((bf16[2,2,32,512]{3,2,1,0:T(8,128)(2,1)S(1)}, bf16[2,2,32,512]{3,2,1,0:T(8,128)(2,1)S(1)}, u32[]{:S(2)}, u32[]{:S(2)}) %collective-permute-start.1) | collective-permute-done | bytes 131104 | tf_op jit(solution)/shard_map/ppermute | solution.py:157
  31.0 0.9 %collective-permute-start.3 = (bf16[2,2,32,512]{3,2,1,0:T(8,128)(2,1)S(1)}, bf16[2,2,32,512]{3,2,1,0:T(8,128)(2,1)S(1)}, u32[]{:S(2)}, u32[]{:S(2)}) collective-permute-start(bf16[2,2,32,512]{3,2,1,0:T(8,128)(2,1)S(1)} %collective-permute-done.1.direct), channel_id=1, source_target_pairs={{0,1},{1,0},{2,3},{3,2},{4,5},{5,4},{6,7},{7,6},{8,9},{9,8},{10,11... | collective-permute-start | bytes 393224 | tf_op jit(solution)/shard_map/ppermute | solution.py:157
  31.9 1.0 %collective-permute-done.3.passed = bf16[2,2,32,512]{3,2,1,0:T(8,128)(2,1)S(1)} collective-permute-done((bf16[2,2,32,512]{3,2,1,0:T(8,128)(2,1)S(1)}, bf16[2,2,32,512]{3,2,1,0:T(8,128)(2,1)S(1)}, u32[]{:S(2)}, u32[]{:S(2)}) %collective-permute-start.3) | collective-permute-done | bytes 131104 | tf_op jit(solution)/shard_map/ppermute | solution.py:157
  32.9 6.0 %all-to-all-done = bf16[128,16,128]{2,1,0:T(8,128)(2,1)S(1)} async-done(((bf16[128,16,128]{2,1,0:T(8,128)(2,1)}), bf16[128,16,128]{2,1,0:T(8,128)(2,1)S(1)}, u32[]{:S(2)}, u32[]{:S(2)}) %all-to-all-start) | async-done | bytes 524320 | tf_op jit(solution)/shard_map/all_to_all | solution.py:180
  38.9 0.7 select.1
  39.6 17.5 %all_to_all.10 = bf16[16,256,128]{2,1,0:T(8,128)(2,1)S(1)} all-to-all(bf16[16,256,128]{2,1,0:T(8,128)(2,1)S(1)} %bitcast.4), channel_id=1, replica_groups={{0,4,8,12,16,20,24,28,32,36,40,44,48,52,56,60},{64,68,72,76,80,84,88,92..., dimensions={0} | all-to-all | bytes 2097152 | tf_op jit(solution)/shard_map/all_to_all | solution.py:208
  57.1 1.7 %attend_far.1 = bf16[2,2,32,512]{3,2,1,0:T(8,128)(2,1)S(1)} custom-call(s32[136]{0:T(256)S(1)} %plan_sources.1.table, bf16[16,8,2,16,128]{4,3,2,1,0:T(8,128)(2,1)S(1)} %bitcast.6, bf16[2,2,32,512]{3,2,1,0:T(8,128)(2,1)S(1)} %collective-permute-done.1.direct, bf16[2,2,32,512]{3,2,1,0:T(8,128)(2,1)S(1)} %collective-permute-done.3.passed), custom_call_target="tpu_custom_call" | custom-call | flops 400000000 | bytes 1500000 | tf_op jit(solution)/shard_map/attend_far/pallas_call | solution.py:163
  58.8 0.2 collective-permute-start.4
  59.0 1.7 %attend_near.1 = (bf16[2,32,512]{2,1,0:T(8,128)(2,1)S(1)}, bf16[2,32,512]{2,1,0:T(8,128)(2,1)S(1)}) custom-call(s32[136]{0:T(256)S(1)} %plan_sources.1.table, bf16[16,8,2,16,128]{4,3,2,1,0:T(8,128)(2,1)S(1)} %bitcast.7, bf16[2,32,512]{2,1,0:T(8,128)(2,1)S(1)} %get-tuple-element.37.own, bf16[2,32,512]{2,1,0:T(8,128)(2,1)S(1)} %collective-permute-done.2.near), custom_call_target="tpu_custom_call" | custom-call | flops 400000000 | bytes 1500000 | tf_op jit(solution)/shard_map/attend_near/pallas_call | solution.py:163
  60.7 4.2 %collective-permute-start.5 = (bf16[2,32,512]{2,1,0:T(8,128)(2,1)S(1)}, bf16[2,32,512]{2,1,0:T(8,128)(2,1)S(1)}, u32[]{:S(2)}, u32[]{:S(2)}) collective-permute-start(bf16[2,32,512]{2,1,0:T(8,128)(2,1)S(1)} %get-tuple-element.40), channel_id=1, source_target_pairs={{0,1},{1,0},{2,3},{3,2},{4,5},{5,4},{6,7},{7,6},{8,9},{9,8},{10,11... | collective-permute-start | bytes 196616 | tf_op jit(solution)/shard_map/ppermute | solution.py:157
  64.9 0.9 %collective-permute-done.5.near = bf16[2,32,512]{2,1,0:T(8,128)(2,1)S(1)} collective-permute-done((bf16[2,32,512]{2,1,0:T(8,128)(2,1)S(1)}, bf16[2,32,512]{2,1,0:T(8,128)(2,1)S(1)}, u32[]{:S(2)}, u32[]{:S(2)}) %collective-permute-start.5) | collective-permute-done | bytes 65568 | tf_op jit(solution)/shard_map/ppermute | solution.py:157
  65.8 0.0 collective-permute-done.4.direct
  65.8 2.7 %collective-permute-start.6 = (bf16[2,2,32,512]{3,2,1,0:T(8,128)(2,1)S(1)}, bf16[2,2,32,512]{3,2,1,0:T(8,128)(2,1)S(1)}, u32[]{:S(2)}, u32[]{:S(2)}) collective-permute-start(bf16[2,2,32,512]{3,2,1,0:T(8,128)(2,1)S(1)} %collective-permute-done.4.direct), channel_id=1, source_target_pairs={{0,1},{1,0},{2,3},{3,2},{4,5},{5,4},{6,7},{7,6},{8,9},{9,8},{10,11... | collective-permute-start | bytes 393224 | tf_op jit(solution)/shard_map/ppermute | solution.py:157
  68.6 1.0 %collective-permute-done.6.passed = bf16[2,2,32,512]{3,2,1,0:T(8,128)(2,1)S(1)} collective-permute-done((bf16[2,2,32,512]{3,2,1,0:T(8,128)(2,1)S(1)}, bf16[2,2,32,512]{3,2,1,0:T(8,128)(2,1)S(1)}, u32[]{:S(2)}, u32[]{:S(2)}) %collective-permute-start.6) | collective-permute-done | bytes 131104 | tf_op jit(solution)/shard_map/ppermute | solution.py:157
  69.6 0.7 %place.1 = (bf16[32,2048]{1,0:T(8,128)(2,1)}, bf16[32,2048]{1,0:T(8,128)(2,1)}) custom-call(bf16[2,32,512]{2,1,0:T(8,128)(2,1)S(1)} %get-tuple-element.41.own, bf16[2,32,512]{2,1,0:T(8,128)(2,1)S(1)} %collective-permute-done.5.near, bf16[2,2,32,512]{3,2,1,0:T(8,128)(2,1)S(1)} %collective-permute-done.4.direct, ...), custom_call_target="tpu_custom_call" | custom-call | tf_op jit(solution)/shard_map/place/pallas_call | solution.py:163
Async XLA Ops:
  0.6 5.9 %copy-start.5 = (bf16[32,512]{1,0:T(8,128)(2,1)S(1)}, bf16[32,512]{1,0:T(8,128)(2,1)}, u32[]{:S(2)}) copy-start(bf16[32,512]{1,0:T(8,128)(2,1)} %dv.3) | copy-start | bytes 98308
  0.6 5.9 %copy-start.4 = (bf16[32,512]{1,0:T(8,128)(2,1)S(1)}, bf16[32,512]{1,0:T(8,128)(2,1)}, u32[]{:S(2)}) copy-start(bf16[32,512]{1,0:T(8,128)(2,1)} %dk.3) | copy-start | bytes 98308
  0.7 5.9 %copy-start.3 = (bf16[32,512]{1,0:T(8,128)(2,1)S(1)}, bf16[32,512]{1,0:T(8,128)(2,1)}, u32[]{:S(2)}) copy-start(bf16[32,512]{1,0:T(8,128)(2,1)} %v.3) | copy-start | bytes 98308
  0.7 5.8 %copy-start.2 = (bf16[32,512]{1,0:T(8,128)(2,1)S(1)}, bf16[32,512]{1,0:T(8,128)(2,1)}, u32[]{:S(2)}) copy-start(bf16[32,512]{1,0:T(8,128)(2,1)} %k.3) | copy-start | bytes 98308
  2.1 4.4 %collective-permute-start = (bf16[2,4,32,128]{3,2,1,0:T(8,128)(2,1)}, bf16[2,4,32,128]{3,2,1,0:T(8,128)(2,1)S(1)}, u32[]{:S(2)}, u32[]{:S(2)}) collective-permute-start(bf16[2,4,32,128]{3,2,1,0:T(8,128)(2,1)} %pack_keys.1), channel_id=1, source_target_pairs={{0,1},{1,0},{2,3},{3,2},{4,5},{5,4},{6,7},{7,6},{8,9},{9,8},{10,11... | collective-permute-start | bytes 196616 | tf_op jit(solution)/shard_map/ppermute | solution.py:157
  7.4 13.9 %copy-start = (bf16[32,2048]{1,0:T(8,128)(2,1)S(1)}, bf16[32,2048]{1,0:T(8,128)(2,1)}, u32[]{:S(2)}) copy-start(bf16[32,2048]{1,0:T(8,128)(2,1)} %q.1) | copy-start | bytes 393220
  7.4 13.9 %copy-start.1 = (bf16[32,2048]{1,0:T(8,128)(2,1)S(1)}, bf16[32,2048]{1,0:T(8,128)(2,1)}, u32[]{:S(2)}) copy-start(bf16[32,2048]{1,0:T(8,128)(2,1)} %dq.1) | copy-start | bytes 393220
  7.4 31.5 %all-to-all-start = ((bf16[128,16,128]{2,1,0:T(8,128)(2,1)}), bf16[128,16,128]{2,1,0:T(8,128)(2,1)S(1)}, u32[]{:S(2)}, u32[]{:S(2)}) async-start(bf16[128,16,128]{2,1,0:T(8,128)(2,1)} %bitcast), calls=%async_computation | async-start | bytes 1048576 | tf_op jit(solution)/shard_map/all_to_all | solution.py:180
  21.5 3.1 %copy-start.6 = (s32[64]{0:T(128)S(1)}, s32[64]{0:T(128)}, u32[]{:S(2)}) copy-start(s32[64]{0:T(128)} %plan.1) | copy-start | bytes 772
  21.5 3.1 %copy-start.7 = (s32[64]{0:T(128)S(1)}, s32[64]{0:T(128)}, u32[]{:S(2)}) copy-start(s32[64]{0:T(128)} %docs.1) | copy-start | bytes 772
  21.6 5.4 %collective-permute-start.2 = (bf16[2,32,512]{2,1,0:T(8,128)(2,1)S(1)}, bf16[2,32,512]{2,1,0:T(8,128)(2,1)S(1)}, u32[]{:S(2)}, u32[]{:S(2)}) collective-permute-start(bf16[2,32,512]{2,1,0:T(8,128)(2,1)S(1)} %get-tuple-element.24), channel_id=1, source_target_pairs={{0,1},{1,0},{2,3},{3,2},{4,5},{5,4},{6,7},{7,6},{8,9},{9,8},{10,11... | collective-permute-start | bytes 196616 | tf_op jit(solution)/shard_map/ppermute | solution.py:157
  22.3 8.7 %collective-permute-start.1 = (bf16[2,2,32,512]{3,2,1,0:T(8,128)(2,1)S(1)}, bf16[2,2,32,512]{3,2,1,0:T(8,128)(2,1)S(1)}, u32[]{:S(2)}, u32[]{:S(2)}) collective-permute-start(bf16[2,2,32,512]{3,2,1,0:T(8,128)(2,1)S(1)} %get-tuple-element.23), channel_id=1, source_target_pairs={{0,2},{1,3},{2,0},{3,1},{4,6},{5,7},{6,4},{7,5},{8,10},{9,11},{10,... | collective-permute-start | bytes 393224 | tf_op jit(solution)/shard_map/ppermute | solution.py:157
  31.0 1.9 %collective-permute-start.3 = (bf16[2,2,32,512]{3,2,1,0:T(8,128)(2,1)S(1)}, bf16[2,2,32,512]{3,2,1,0:T(8,128)(2,1)S(1)}, u32[]{:S(2)}, u32[]{:S(2)}) collective-permute-start(bf16[2,2,32,512]{3,2,1,0:T(8,128)(2,1)S(1)} %collective-permute-done.1.direct), channel_id=1, source_target_pairs={{0,1},{1,0},{2,3},{3,2},{4,5},{5,4},{6,7},{7,6},{8,9},{9,8},{10,11... | collective-permute-start | bytes 393224 | tf_op jit(solution)/shard_map/ppermute | solution.py:157
  58.8 7.0 %collective-permute-start.4 = (bf16[2,2,32,512]{3,2,1,0:T(8,128)(2,1)S(1)}, bf16[2,2,32,512]{3,2,1,0:T(8,128)(2,1)S(1)}, u32[]{:S(2)}, u32[]{:S(2)}) collective-permute-start(bf16[2,2,32,512]{3,2,1,0:T(8,128)(2,1)S(1)} %attend_far.1), channel_id=1, source_target_pairs={{0,2},{1,3},{2,0},{3,1},{4,6},{5,7},{6,4},{7,5},{8,10},{9,11},{10,... | collective-permute-start | bytes 393224 | tf_op jit(solution)/shard_map/ppermute | solution.py:157
  60.7 5.1 %collective-permute-start.5 = (bf16[2,32,512]{2,1,0:T(8,128)(2,1)S(1)}, bf16[2,32,512]{2,1,0:T(8,128)(2,1)S(1)}, u32[]{:S(2)}, u32[]{:S(2)}) collective-permute-start(bf16[2,32,512]{2,1,0:T(8,128)(2,1)S(1)} %get-tuple-element.40), channel_id=1, source_target_pairs={{0,1},{1,0},{2,3},{3,2},{4,5},{5,4},{6,7},{7,6},{8,9},{9,8},{10,11... | collective-permute-start | bytes 196616 | tf_op jit(solution)/shard_map/ppermute | solution.py:157
  65.8 3.7 %collective-permute-start.6 = (bf16[2,2,32,512]{3,2,1,0:T(8,128)(2,1)S(1)}, bf16[2,2,32,512]{3,2,1,0:T(8,128)(2,1)S(1)}, u32[]{:S(2)}, u32[]{:S(2)}) collective-permute-start(bf16[2,2,32,512]{3,2,1,0:T(8,128)(2,1)S(1)} %collective-permute-done.4.direct), channel_id=1, source_target_pairs={{0,1},{1,0},{2,3},{3,2},{4,5},{5,4},{6,7},{7,6},{8,9},{9,8},{10,11... | collective-permute-start | bytes 393224 | tf_op jit(solution)/shard_map/ppermute | solution.py:157
